TPU v7x, 256 devices: a whole 4x4x8 slice. The times are simulated.
256 devices in a mesh: leaf: 256 (over y, z, x, core).
Axes of the slice: x: 4, y: 4, z: 8, core: 2. Of those that a mesh axis runs over, the one named last changes fastest.
Arguments:
- white_noise: float32 [262144, 128], P('leaf'), may hold values from -6 to 6
- leaf_inverse: float32 [262144, 1024], P('leaf'), may hold values from -1 to 4, as said below
- bases: float32 [262144, 1024], P('leaf'), may hold values from -2 to 2
Outputs:
- solution: float32 [262144, 128], P('leaf')
Inputs may be any that keep to these rules, and one draw needn't show every extreme that they name: `leaf_inverse`: each leaf's block of 1024 rows is symmetric positive definite.
All inputs are finite; a program needn't handle non-finite values.
Results may differ from a plain program's by a relative error of at most 0.0001.
Values sent between devices are 32-bit elements; how exact they have to be, the bound alone decides.
No kernel may reach another device: no remote copies, remote signals or barrier semaphores. Data moves between devices by JAX's collectives and lax.ppermute only.
A program may use at most 128 MiB of HBM per device.

v0:
```python
import jax
import jax.numpy as jnp
from jax import lax
from jax.experimental import pallas as pl
from jax.experimental.pallas import tpu as pltpu
from jax.sharding import PartitionSpec as P


R = 128
HALF = R // 2
QUARTER = HALF // 4
LEVELS = 8
F32 = jnp.float32
CORE_MASK = 1
TURNS = 8
RING_MASKS = (2, 4, 6)


def swap(value, mask):
    return lax.ppermute(value, "leaf", [(i, i ^ mask) for i in range(lax.axis_size("leaf"))])


def split(v):
    high = v.astype(jnp.bfloat16)
    return high, (v - high.astype(F32)).astype(jnp.bfloat16)


def dot_split(a, b, contract=(1, 0)):
    dims = (((contract[0],), (contract[1],)), ((), ()))

    def one(p, q):
        return lax.dot_general(p, q, dims, preferred_element_type=F32)

    return one(a[0], b[0]) + (one(a[0], b[1]) + one(a[1], b[0]))


def cols(parts, start, stop):
    return tuple(part[:, start:stop] for part in parts)


def row_blocks(first):
    offset = 0
    out = []
    for m in range(first, LEVELS):
        width = (LEVELS + 1 - m) * R
        out.append((m, offset, width))
        offset += width
    return out, offset


def spd_inverse(rows):
    shape = (8, R)
    sub = lax.broadcasted_iota(jnp.int32, shape, 0)
    lane = lax.broadcasted_iota(jnp.int32, shape, 1)

    def spread_row(v, i):
        return jnp.broadcast_to(v[i : i + 1, :], shape)

    def spread_col(v, k):
        return jnp.broadcast_to(v[:, k : k + 1], shape)

    count = R // 8
    turns = TURNS
    per_turn = count // turns

    def eliminate(rows, p):
        rows = list(rows)
        panel = rows[p]
        base = 8 * p
        panel_rows = [spread_row(panel, j) for j in range(8)]
        d = [spread_col(panel, base + j) for j in range(8)]
        for a in range(0, 8, 2):
            b = a + 1
            ra = [spread_row(d[j], a) for j in range(8)]
            rb = [spread_row(d[j], b) for j in range(8)]
            inv_det = 1.0 / (ra[a] * rb[b] - ra[b] * rb[a])
            ma, mb = sub == a, sub == b
            ca, cb = d[a], d[b]
            ta = (ca * rb[b] - cb * rb[a]) * inv_det
            tb = (cb * ra[a] - ca * ra[b]) * inv_det
            iaa, iab = rb[b] * inv_det, -(ra[b] * inv_det)
            iba, ibb = -(rb[a] * inv_det), ra[a] * inv_det
            for j in range(8):
                if j == a:
                    d[j] = jnp.where(ma, iaa, jnp.where(mb, iba, -ta))
                elif j == b:
                    d[j] = jnp.where(ma, iab, jnp.where(mb, ibb, -tb))
                else:
                    na = iaa * ra[j] + iab * rb[j]
                    nb = iba * ra[j] + ibb * rb[j]
                    d[j] = jnp.where(ma, na, jnp.where(mb, nb, d[j] - (ta * ra[j] + tb * rb[j])))
        inside = (lane >= base) & (lane < base + 8)
        panel = None
        for j in range(8):
            term = d[j] * jnp.where(inside, jnp.where(lane == base + j, 1.0, 0.0), panel_rows[j])
            panel = term if panel is None else panel + term
        rows[p] = panel
        spread = [spread_row(panel, j) for j in range(8)]
        for step in range(1, count):
            i = (p + step) % count
            c = rows[i]
            total = None
            for j in range(0, 8, 2):
                pair = spread_col(c, base + j) * spread[j] + spread_col(c, base + j + 1) * spread[j + 1]
                total = pair if total is None else total + pair
            rows[i] = jnp.where(inside, 0.0, c) - total
        return rows

    def turn(_, rows):
        for p in range(per_turn):
            rows = eliminate(rows, p)
        rows = rows[per_turn:] + rows[:per_turn]
        return tuple(pltpu.roll(row, R - 8 * per_turn, 1) for row in rows)

    return list(lax.fori_loop(0, turns, turn, tuple(rows)))


def vmem(n):
    return [pl.BlockSpec(memory_space=pltpu.VMEM)] * n


def smem():
    return [pl.BlockSpec(memory_space=pltpu.SMEM)]


def out(*shape):
    return jax.ShapeDtypeStruct(shape, F32)


def call(kernel, outs, args, index=None, scratch=(), flops=0):
    moved = 4 * (sum(a.size for a in args) + sum(o.size for o in outs))
    head = [] if index is None else [index]
    return pl.pallas_call(
        kernel,
        out_shape=outs,
        in_specs=(smem() if head else []) + vmem(len(args)),
        out_specs=vmem(len(outs)),
        scratch_shapes=list(scratch),
        cost_estimate=pl.CostEstimate(flops=flops, bytes_accessed=moved, transcendentals=0),
        compiler_params=pltpu.CompilerParams(vmem_limit_bytes=16 << 20),
    )(*head, *args)


HEAD = 3 * R
CHUNK = 256


def head_kernel(
    index_ref, a_hbm, u_hbm, w_hbm, x_ref, rows_ref, keep_ref, send_ref, a, u, w, u_high, u_low, row2, a_sem, sem
):
    core = index_ref[0] & 1
    chunks = a.shape[0]
    copies = [
        pltpu.make_async_copy(u_hbm.at[:, :HEAD], u.at[:, :HEAD], sem.at[0]),
        pltpu.make_async_copy(u_hbm.at[:, HEAD:], u.at[:, HEAD:], sem.at[1]),
        pltpu.make_async_copy(w_hbm, w, sem.at[2]),
    ]

    def a_copy(r):
        return pltpu.make_async_copy(a_hbm.at[pl.ds(r * CHUNK, CHUNK), :], a.at[r], a_sem.at[r])

    copies[0].start()
    a_copy(0).start()
    copies[1].start()
    copies[2].start()
    for r in range(1, chunks):
        a_copy(r).start()
    copies[0].wait()
    u_high[...], u_low[...] = split(u[:, :HEAD])
    rows_ref[...] = jnp.zeros_like(rows_ref)
    row2[...] = jnp.zeros_like(row2)

    @pl.loop(0, chunks)
    def _(r):
        a_copy(r).wait()
        span = pl.ds(pl.multiple_of(r * CHUNK, CHUNK), CHUNK)
        x = dot_split(split(a[r]), (u_high[...], u_low[...]))
        x_ref[span, :] = x

        @pl.when(r == 0)
        def _():
            copies[1].wait()
            copies[2].wait()

        x = split(x)
        chunk_u, chunk_w = split(u[span, :]), split(w[span, :])
        at = 0
        for m in range(3):
            left = cols(x, m * R, (m + 1) * R)
            width = (LEVELS - m) * R
            piece = dot_split(left, cols(chunk_u, m * R, LEVELS * R), (0, 0))
            noise = dot_split(left, chunk_w, (0, 0))
            if m < 2:
                rows_ref[:, at : at + width] += piece
                rows_ref[:, at + width : at + width + R] += noise
                at += width + R
            else:
                row2[:, :width] += piece
                row2[:, width:] += noise

    keep_ref[...] = jnp.where(core == 0, row2[:HALF, :], row2[HALF:, :])
    send_ref[...] = jnp.where(core == 0, row2[HALF:, :], row2[:HALF, :])


def head(index, leaf_inverse, bases, white_noise):
    leaf = leaf_inverse.shape[0]
    n2 = (LEVELS - 1) * R
    return pl.pallas_call(
        head_kernel,
        name="head",
        out_shape=(out(leaf, HEAD), out(R, 17 * R), out(HALF, n2), out(HALF, n2)),
        in_specs=smem() + [pl.BlockSpec(memory_space=pltpu.HBM)] * 3,
        out_specs=vmem(4),
        scratch_shapes=[
            pltpu.VMEM((leaf // CHUNK, CHUNK, leaf), F32),
            pltpu.VMEM((leaf, LEVELS * R), F32),
            pltpu.VMEM((leaf, R), F32),
            pltpu.VMEM((leaf, HEAD), jnp.bfloat16),
            pltpu.VMEM((leaf, HEAD), jnp.bfloat16),
            pltpu.VMEM((R, n2), F32),
            pltpu.SemaphoreType.DMA((leaf // CHUNK,)),
            pltpu.SemaphoreType.DMA((3,)),
        ],
        cost_estimate=pl.CostEstimate(flops=6 * leaf * R * 54 * R, bytes_accessed=8 * leaf * leaf, transcendentals=0),
        compiler_params=pltpu.CompilerParams(vmem_limit_bytes=24 << 20),
    )(index, leaf_inverse, bases, white_noise)


def tail_solve_kernel(a_ref, u_ref, w_ref, x_ref, high_ref, low_ref):
    tail = (LEVELS - 3) * R
    high_ref[:, :tail], low_ref[:, :tail] = split(u_ref[:, 3 * R :])
    high_ref[:, tail:], low_ref[:, tail:] = split(w_ref[...])

    @pl.loop(0, 4)
    def _(r):
        rows = pl.ds(pl.multiple_of(r * 2 * R, 2 * R), 2 * R)
        x_ref[rows, :] = dot_split(split(a_ref[rows, :]), (high_ref[...], low_ref[...]))


def rest_rows_kernel(index_ref, u_ref, x_ref, keep_ref, send_ref):
    core = index_ref[0] & 1
    x = split(x_ref[...])
    for m, at, width in row_blocks(3)[0]:
        u = split(u_ref[:, m * R : (m + 1) * R])
        piece = dot_split(u, cols(x, (m - 3) * R, (LEVELS - 2) * R), (0, 0))
        keep_ref[:, at : at + width] = jnp.where(core == 0, piece[:HALF], piece[HALF:])
        send_ref[:, at : at + width] = jnp.where(core == 0, piece[HALF:], piece[:HALF])


def invert_store(panel_ref, w_ref):
    rows = [panel_ref[8 * i : 8 * i + 8, :R] for i in range(R // 8)]
    sub = lax.broadcasted_iota(jnp.int32, (8, R), 0)
    lane = lax.broadcasted_iota(jnp.int32, (8, R), 1)
    rows = [row + jnp.where(lane == sub + 8 * i, 1.0, 0.0) for i, row in enumerate(rows)]
    inverse = split(jnp.concatenate(spd_inverse(rows), axis=0))
    w_ref[...] = dot_split(inverse, split(panel_ref[:, R:]))


def invert_sum_kernel(own_ref, got_ref, panel_ref, w_ref):
    n = panel_ref.shape[1]
    panel_ref[...] = own_ref[:, :n] + got_ref[:, :n]
    invert_store(panel_ref, w_ref)


def invert_half_kernel(index_ref, own_ref, got_ref, panel_ref, w_ref):
    core = index_ref[0] & 1
    own, got = own_ref[...], got_ref[...]
    panel_ref[:HALF, :] = jnp.where(core == 0, own, got)
    panel_ref[HALF:, :] = jnp.where(core == 0, got, own)
    invert_store(panel_ref, w_ref)


def invert_ring_kernel(index_ref, own_ref, got_ref, panel_ref, w_ref):
    core = index_ref[0] & 1
    x = (index_ref[0] >> 1) & 3
    for k in range(4):
        at = QUARTER * jnp.bitwise_xor(x, k)
        mine = pl.multiple_of(core * HALF + at, QUARTER)
        other = pl.multiple_of((1 - core) * HALF + at, QUARTER)
        panel_ref[pl.ds(mine, QUARTER), :] = own_ref[k]
        panel_ref[pl.ds(other, QUARTER), :] = got_ref[k]
    invert_store(panel_ref, w_ref)


def invert(level, own, got, index):
    n = (LEVELS + 1 - level) * R
    outs = (out(R, n), out(R, n - R))
    flops = 6 * R * R * n + 2 * R * R * R * 40
    if level == 0:
        return call(invert_sum_kernel, outs, (own, got), flops=flops)
    kernel = invert_ring_kernel if 3 <= level <= 5 else invert_half_kernel
    return call(kernel, outs, (own, got), index=index, flops=flops)


def row1_kernel(index_ref, own_ref, got_ref, keep_ref, got2_ref, panel_ref, w_ref, row_ref, half_ref, half2_ref):
    core = index_ref[0] & 1
    w = split(w_ref[...])
    row = own_ref[:, 9 * R :] + got_ref[:, 9 * R :] - dot_split(split(panel_ref[:, R : 2 * R]), w, (0, 0))
    row_ref[...] = row
    half_ref[...] = jnp.where(core == 0, row[:HALF], row[HALF:])
    change = dot_split(split(panel_ref[:, 2 * R : 3 * R]), cols(w, R, LEVELS * R), (0, 0))
    half2_ref[...] = keep_ref[...] + got2_ref[...] - jnp.where(core == 0, change[:HALF], change[HALF:])


def ahead_kernel(index_ref, own_ref, got_ref, panel_ref, w_ref, half_ref):
    core = index_ref[0] & 1
    change = dot_split(split(panel_ref[:, R : 2 * R]), split(w_ref[...]), (0, 0))
    half_ref[...] = own_ref[...] + got_ref[...] - jnp.where(core == 0, change[:HALF], change[HALF:])


def downdate(core, level, panel_ref, w_ref, rows):
    w = split(w_ref[...])
    for m, offset, width in rows:
        left = split(panel_ref[:, (m - level) * R : (m - level + 1) * R])
        full = dot_split(left, cols(w, (m - level - 1) * R, (LEVELS - level) * R), (0, 0))
        yield m, offset, width, jnp.where(core == 0, full[:HALF], full[HALF:])


def rest0_kernel(index_ref, own_ref, got_ref, panel_ref, w_ref, rest_ref):
    core = index_ref[0] & 1
    for m, at, width, change in downdate(core, 0, panel_ref, w_ref, row_blocks(3)[0]):
        span = slice(at, at + width)
        rest_ref[:, span] = own_ref[:, span] + got_ref[:, span] - change


def whole_downdate(level, panel_ref, w_ref, rows, scr):
    w = split(w_ref[...])
    for m, at, width in rows:
        left = split(panel_ref[:, (m - level) * R : (m - level + 1) * R])
        scr[:, at : at + width] = dot_split(left, cols(w, (m - level - 1) * R, (LEVELS - level) * R), (0, 0))


def quarter_at(index_ref, k):
    x = (index_ref[0] >> 1) & 3
    return QUARTER * jnp.bitwise_xor(x, k)


def update1_kernel(index_ref, rest_ref, panel_ref, w_ref, q0, q1, q2, q3, scr):
    core = index_ref[0] & 1
    whole_downdate(1, panel_ref, w_ref, row_blocks(3)[0], scr)
    for k, q in enumerate((q0, q1, q2, q3)):
        at = quarter_at(index_ref, k)
        mine = pl.multiple_of(at, QUARTER)
        both = pl.multiple_of(core * HALF + at, QUARTER)
        q[...] = rest_ref[pl.ds(mine, QUARTER), :] - scr[pl.ds(both, QUARTER), :]


def update_quarter_kernel(level):
    skip = (LEVELS + 1 - level) * R if level > 2 else 0

    def kernel(index_ref, rest_ref, panel_ref, w_ref, out_ref, scr):
        core = index_ref[0] & 1
        whole_downdate(level, panel_ref, w_ref, row_blocks(level + 1)[0], scr)
        at = pl.multiple_of(core * HALF + quarter_at(index_ref, 0), QUARTER)
        out_ref[...] = rest_ref[:, skip:] - scr[pl.ds(at, QUARTER), :]

    return kernel


def store_next(level, m, at, value, row_ref, rest_ref):
    if m == level + 1:
        row_ref[...] = value
    else:
        at -= (LEVELS - level) * R
        rest_ref[:, at : at + value.shape[1]] = value


def update5_kernel(index_ref, own_ref, panel_ref, w_ref, row_ref, rest_ref, scr):
    core = index_ref[0] & 1
    for k in range(4):
        at = pl.multiple_of(quarter_at(index_ref, k), QUARTER)
        scr[pl.ds(at, QUARTER), :] = own_ref[k]
    skip = (LEVELS + 1 - 5) * R
    for m, at, width, change in downdate(core, 5, panel_ref, w_ref, row_blocks(6)[0]):
        store_next(5, m, at, scr[:, skip + at : skip + at + width] - change, row_ref, rest_ref)


def update6_kernel(index_ref, own_ref, got_ref, panel_ref, w_ref, row_ref):
    core = index_ref[0] & 1
    for _, _, _, change in downdate(core, 6, panel_ref, w_ref, row_blocks(7)[0]):
        row_ref[...] = own_ref[...] + got_ref[...] - change


def solve_step_kernel(solved_ref, w_ref, next_ref):
    w = split(w_ref[...])

    @pl.loop(0, solved_ref.shape[0] // CHUNK)
    def _(r):
        span = pl.ds(pl.multiple_of(r * CHUNK, CHUNK), CHUNK)
        next_ref[span, :] = solved_ref[span, R:] - dot_split(split(solved_ref[span, :R]), w)


def solve_step(solved, w):
    rows, n = solved.shape[0], solved.shape[1] - R
    (result,) = call(solve_step_kernel, (out(rows, n),), (solved, w), flops=6 * rows * R * n)
    return result


def solve_four_kernel(head_ref, tail_ref, w0, w1, w2, w3, next_ref, high, low):
    for j, w in ((3, w3), (2, w2), (1, w1), (0, w0)):
        mid = (3 - j) * R
        t = w[:, mid:]
        if j < 3:
            below = slice((j + 1) * R, 4 * R)
            t = t - dot_split(split(w[:, :mid]), (high[below, :], low[below, :]))
        high[j * R : (j + 1) * R, :], low[j * R : (j + 1) * R, :] = split(t)

    @pl.loop(0, head_ref.shape[0] // CHUNK)
    def _(r):
        span = pl.ds(pl.multiple_of(r * CHUNK, CHUNK), CHUNK)
        change = dot_split(split(head_ref[span, :]), (high[:HEAD, :], low[:HEAD, :]))
        change = change + dot_split(split(tail_ref[span, :R]), (high[HEAD:, :], low[HEAD:, :]))
        next_ref[span, :] = tail_ref[span, R:] - change


def update_flops(level):
    return sum(6 * R * R * width for _, _, width in row_blocks(level + 1)[0])


def ring_all(value):
    return jnp.stack([value] + [swap(value, mask) for mask in RING_MASKS])


def tree_solve(white_noise, leaf_inverse, bases):
    index = lax.axis_index("leaf").astype(jnp.int32).reshape(1)
    leaf = leaf_inverse.shape[0]
    x_head, rows01, keep2, send2 = head(index, leaf_inverse, bases, white_noise)
    got01 = swap(rows01, CORE_MASK)
    got2 = swap(send2, CORE_MASK)
    weights = []
    panel, w = invert(0, rows01, got01, index)
    weights.append(w)
    row1, half, half2 = call(
        row1_kernel,
        (out(R, 8 * R), out(HALF, 8 * R), out(HALF, 7 * R)),
        (rows01, got01, keep2, got2, panel, w),
        index=index,
        flops=90 * R**3,
    )
    got = swap(half, 2)
    (x_tail,) = call(
        tail_solve_kernel,
        (out(leaf, 6 * R),),
        (leaf_inverse, bases, white_noise),
        scratch=(pltpu.VMEM((leaf, 6 * R), jnp.bfloat16),) * 2,
        flops=6 * leaf * leaf * 6 * R,
    )
    width3 = row_blocks(3)[1]
    keep, send = call(
        rest_rows_kernel,
        (out(HALF, width3), out(HALF, width3)),
        (bases, x_tail),
        index=index,
        flops=6 * leaf * R * width3,
    )
    got_rest = swap(send, CORE_MASK)
    (rest,) = call(rest0_kernel, (out(HALF, width3),), (keep, got_rest, panel, w), index=index, flops=update_flops(2))
    half2_after, got = lax.optimization_barrier((half2, got))
    got2 = swap(half2_after, 2)
    half = half + got
    panel, w = invert(1, half, swap(half, CORE_MASK), index)
    weights.append(w)
    (half,) = call(ahead_kernel, (out(HALF, 7 * R),), (half2, got2, panel, w), index=index, flops=42 * R**3)
    got = swap(half, 4)
    quarters = call(
        update1_kernel,
        (out(QUARTER, width3),) * 4,
        (rest, row1, w),
        index=index,
        scratch=(pltpu.VMEM((R, width3), F32),),
        flops=update_flops(2),
    )
    quarters, got = lax.optimization_barrier((quarters, got))
    half = half + got
    other = swap(half, CORE_MASK)
    panel, w = invert(2, half, other, index)
    weights.append(w)
    rest = quarters[0]
    for k in (1, 2, 0):
        part = swap(quarters[1 + k], RING_MASKS[k])
        rest = rest + part
    for level in range(2, 6):
        width = (LEVELS + 1 - level) * R
        if level > 2:
            rest = rest + swap(rest, 1 << level)
            if level < 5:
                row = ring_all(rest[:, :width])
            else:
                rest = ring_all(rest)
                row = rest[:, :, :width]
            panel, w = invert(level, row, swap(row, CORE_MASK), index)
            weights.append(w)
        next_width = row_blocks(level + 1)[1]
        if level < 5:
            (rest,) = call(
                update_quarter_kernel(level),
                (out(QUARTER, next_width),),
                (rest, panel, w),
                index=index,
                scratch=(pltpu.VMEM((R, next_width), F32),),
                flops=update_flops(level),
            )
        else:
            half, rest = call(
                update5_kernel,
                (out(HALF, 3 * R), out(HALF, 2 * R)),
                (rest, panel, w),
                index=index,
                scratch=(pltpu.VMEM((HALF, 9 * R), F32),),
                flops=update_flops(level),
            )
        if level == 3:
            (solved,) = call(
                solve_four_kernel,
                (out(leaf, 5 * R),),
                (x_head, x_tail, *weights),
                scratch=(pltpu.VMEM((4 * R, 5 * R), jnp.bfloat16),) * 2,
                flops=6 * leaf * 4 * R * 5 * R,
            )
        elif level > 3:
            solved = solve_step(solved, w)
    got, got_rest = swap(half, 64), swap(rest, 64)
    half = half + got
    panel, w = invert(6, half, swap(half, CORE_MASK), index)
    solved = solve_step(solved, w)
    (half,) = call(update6_kernel, (out(HALF, 2 * R),), (rest, got_rest, panel, w), index=index, flops=update_flops(6))
    half = half + swap(half, 128)
    _, w = invert(7, half, swap(half, CORE_MASK), index)
    return solve_step(solved, w)


def solution(mesh):
    in_specs = (P("leaf", None), P("leaf", None), P("leaf", None))
    out_specs = P("leaf", None)
    return jax.shard_map(tree_solve, mesh=mesh, in_specs=in_specs, out_specs=out_specs, check_vma=False)
```

profile of v0, /device:TPU:10, one launch (start us, length us, event | category | flops | bytes accessed | tf_op | source)
XLA Modules:
  0.0 168.2 jit_solution(10414023460639237101)
XLA Ops:
  5.4 9.1 %head.1 = (f32[1024,384]{1,0:T(8,128)S(1)}, f32[128,2176]{1,0:T(8,128)S(1)}, f32[64,896]{1,0:T(8,128)S(1)}, f32[64,896]{1,0:T(8,128)S(1)}) custom-call(s32[1]{0:T(128)} %bitcast.index_ref, f32[1024,1024]{1,0:T(8,128)S(1)} %copy-done, f32[1024,1024]{1,0:T(8,128)S(1)} %copy-done.2, f32[1024,128]{1,0:T(8,128)S(1)} %copy-done.4), custom_call_target="tpu_custom_call" | custom-call | flops 5435817984 | bytes 8388608 | tf_op jit(solution)/shard_map/head/pallas_call | solution.py:208
  15.1 6.2 %shard_map.37.x_ref.tail_ref = f32[1024,768]{1,0:T(8,128)S(1)} custom-call(f32[1024,1024]{1,0:T(8,128)S(1)} %copy-done.1, f32[1024,1024]{1,0:T(8,128)S(1)} %copy-done.3, f32[1024,128]{1,0:T(8,128)S(1)} %copy-done.4), custom_call_target="tpu_custom_call" | custom-call | flops 4831838208 | bytes 12058624 | tf_op jit(solution)/shard_map/pallas_call | solution.py:133
  21.3 5.5 %shard_map.38 = (f32[128,1152]{1,0:T(8,128)S(1)}, f32[128,1024]{1,0:T(8,128)S(1)}) custom-call(f32[128,2176]{1,0:T(8,128)S(1)} %get-tuple-element.43.own_ref, f32[128,2176]{1,0:T(8,128)S(1)} %collective-permute-done.got_ref), custom_call_target="tpu_custom_call" | custom-call | flops 281018368 | bytes 3342336 | tf_op jit(solution)/shard_map/pallas_call | solution.py:133
  28.1 2.6 %shard_map.42 = (f32[64,2560]{1,0:T(8,128)S(1)}, f32[64,2560]{1,0:T(8,128)S(1)}) custom-call(s32[1]{0:T(128)} %bitcast.index_ref, f32[1024,1024]{1,0:T(8,128)S(1)} %copy-done.3, f32[1024,768]{1,0:T(8,128)S(1)} %shard_map.37.x_ref.tail_ref), custom_call_target="tpu_custom_call" | custom-call | flops 2013265920 | bytes 8650752 | tf_op jit(solution)/shard_map/pallas_call | solution.py:133
  30.8 5.1 %collective-permute-done.2 = f32[64,1024]{1,0:T(8,128)S(1)} collective-permute-done((f32[64,1024]{1,0:T(8,128)S(1)}, f32[64,1024]{1,0:T(8,128)S(1)}, u32[]{:S(2)}, u32[]{:S(2)}) %collective-permute-start.2) | collective-permute-done | bytes 262176 | tf_op jit(solution)/shard_map/ppermute | solution.py:20
  37.6 5.5 %shard_map.40 = (f32[128,1024]{1,0:T(8,128)S(1)}, f32[128,896]{1,0:T(8,128)S(1)}) custom-call(s32[1]{0:T(128)} %bitcast.index_ref, f32[64,1024]{1,0:T(8,128)S(1)} %add.30.own_ref, f32[64,1024]{1,0:T(8,128)S(1)} %collective-permute-done.3.got_ref), custom_call_target="tpu_custom_call" | custom-call | flops 268435456 | bytes 1507328 | tf_op jit(solution)/shard_map/pallas_call | solution.py:133
  48.2 4.7 %collective-permute-done.6 = f32[64,896]{1,0:T(8,128)S(1)} collective-permute-done((f32[64,896]{1,0:T(8,128)S(1)}, f32[64,896]{1,0:T(8,128)S(1)}, u32[]{:S(2)}, u32[]{:S(2)}) %collective-permute-start.6) | collective-permute-done | bytes 229408 | tf_op jit(solution)/shard_map/ppermute | solution.py:20
  57.1 2.8 %collective-permute-done.10 = f32[16,2560]{1,0:T(8,128)S(1)} collective-permute-done((f32[16,2560]{1,0:T(8,128)S(1)}, f32[16,2560]{1,0:T(8,128)S(1)}, u32[]{:S(2)}, u32[]{:S(2)}) %collective-permute-start.10) | collective-permute-done | bytes 163872 | tf_op jit(solution)/shard_map/ppermute | solution.py:20
  62.7 5.5 %shard_map.45 = (f32[128,896]{1,0:T(8,128)S(1)}, f32[128,768]{1,0:T(8,128)S(1)}) custom-call(s32[1]{0:T(128)} %bitcast.index_ref, f32[64,896]{1,0:T(8,128)S(1)} %add.31.own_ref, f32[64,896]{1,0:T(8,128)S(1)} %collective-permute-done.7.got_ref), custom_call_target="tpu_custom_call" | custom-call | flops 255852544 | bytes 1310720 | tf_op jit(solution)/shard_map/pallas_call | solution.py:133
  70.9 3.4 %collective-permute-done.11 = f32[16,2560]{1,0:T(8,128)S(1)} collective-permute-done((f32[16,2560]{1,0:T(8,128)S(1)}, f32[16,2560]{1,0:T(8,128)S(1)}, u32[]{:S(2)}, u32[]{:S(2)}) %collective-permute-start.11) | collective-permute-done | bytes 163872 | tf_op jit(solution)/shard_map/ppermute | solution.py:20
  75.6 2.9 %collective-permute-start.13 = (f32[16,768]{1,0:T(8,128)S(1)}, f32[16,768]{1,0:T(8,128)S(1)}, u32[]{:S(2)}, u32[]{:S(2)}) collective-permute-start(f32[16,768]{1,0:T(8,128)S(1)} %get-tuple-element.80), channel_id=1, source_target_pairs={{0,4},{1,5},{2,6},{3,7},{4,0},{5,1},{6,2},{7,3},{8,12},{9,13},{10,... | collective-permute-start | bytes 147464 | tf_op jit(solution)/shard_map/ppermute | solution.py:20
  78.5 2.6 %collective-permute-done.13 = f32[16,768]{1,0:T(8,128)S(1)} collective-permute-done((f32[16,768]{1,0:T(8,128)S(1)}, f32[16,768]{1,0:T(8,128)S(1)}, u32[]{:S(2)}, u32[]{:S(2)}) %collective-permute-start.13) | collective-permute-done | bytes 49184 | tf_op jit(solution)/shard_map/ppermute | solution.py:20
  84.1 5.4 %shard_map.47 = (f32[128,768]{1,0:T(8,128)S(1)}, f32[128,640]{1,0:T(8,128)S(1)}) custom-call(s32[1]{0:T(128)} %bitcast.index_ref, f32[4,16,768]{2,1,0:T(8,128)S(1)} %pad_maximum_fusion.1.own_ref, f32[4,16,768]{2,1,0:T(8,128)S(1)} %collective-permute-done.15.got_ref), custom_call_target="tpu_custom_call" | custom-call | flops 243269632 | bytes 1114112 | tf_op jit(solution)/shard_map/pallas_call | solution.py:133
  90.1 3.4 %collective-permute-start.16 = (f32[16,1792]{1,0:T(8,128)S(1)}, f32[16,1792]{1,0:T(8,128)S(1)}, u32[]{:S(2)}, u32[]{:S(2)}) collective-permute-start(f32[16,1792]{1,0:T(8,128)S(1)} %shard_map.49), channel_id=1, source_target_pairs={{0,16},{1,17},{2,18},{3,19},{4,20},{5,21},{6,22},{7,23},{8,24},{9,... | collective-permute-start | bytes 344072 | tf_op jit(solution)/shard_map/ppermute | solution.py:20
  93.5 5.9 %collective-permute-done.16 = f32[16,1792]{1,0:T(8,128)S(1)} collective-permute-done((f32[16,1792]{1,0:T(8,128)S(1)}, f32[16,1792]{1,0:T(8,128)S(1)}, u32[]{:S(2)}, u32[]{:S(2)}) %collective-permute-start.16) | collective-permute-done | bytes 114720 | tf_op jit(solution)/shard_map/ppermute | solution.py:20
  103.6 2.5 %collective-permute-done.18 = f32[16,640]{1,0:T(8,128)S(1)} collective-permute-done((f32[16,640]{1,0:T(8,128)S(1)}, f32[16,640]{1,0:T(8,128)S(1)}, u32[]{:S(2)}, u32[]{:S(2)}) %collective-permute-start.18) | collective-permute-done | bytes 40992 | tf_op jit(solution)/shard_map/ppermute | solution.py:20
  108.2 5.4 %shard_map.50 = (f32[128,640]{1,0:T(8,128)S(1)}, f32[128,512]{1,0:T(8,128)S(1)}) custom-call(s32[1]{0:T(128)} %bitcast.index_ref, f32[4,16,640]{2,1,0:T(8,128)S(1)} %pad_maximum_fusion.2.own_ref, f32[4,16,640]{2,1,0:T(8,128)S(1)} %collective-permute-done.20.got_ref), custom_call_target="tpu_custom_call" | custom-call | flops 230686720 | bytes 917504 | tf_op jit(solution)/shard_map/pallas_call | solution.py:133
  114.0 6.7 %collective-permute-start.21 = (f32[16,1152]{1,0:T(8,128)S(1)}, f32[16,1152]{1,0:T(8,128)S(1)}, u32[]{:S(2)}, u32[]{:S(2)}) collective-permute-start(f32[16,1152]{1,0:T(8,128)S(1)} %shard_map.52), channel_id=1, source_target_pairs={{0,32},{1,33},{2,34},{3,35},{4,36},{5,37},{6,38},{7,39},{8,40},{9,... | collective-permute-start | bytes 221192 | tf_op jit(solution)/shard_map/ppermute | solution.py:20
  120.7 2.6 %collective-permute-done.21 = f32[16,1152]{1,0:T(8,128)S(1)} collective-permute-done((f32[16,1152]{1,0:T(8,128)S(1)}, f32[16,1152]{1,0:T(8,128)S(1)}, u32[]{:S(2)}, u32[]{:S(2)}) %collective-permute-start.21) | collective-permute-done | bytes 73760 | tf_op jit(solution)/shard_map/ppermute | solution.py:20
  132.3 5.4 %shard_map.53 = (f32[128,512]{1,0:T(8,128)S(1)}, f32[128,384]{1,0:T(8,128)S(1)}) custom-call(s32[1]{0:T(128)} %bitcast.index_ref, f32[4,16,512]{2,1,0:T(8,128)S(1)} %slice.14.own_ref, f32[4,16,512]{2,1,0:T(8,128)S(1)} %collective-permute-done.25.got_ref), custom_call_target="tpu_custom_call" | custom-call | flops 218103808 | bytes 720896 | tf_op jit(solution)/shard_map/pallas_call | solution.py:133
  138.5 4.4 %collective-permute-done.26 = f32[64,384]{1,0:T(8,128)S(1)} collective-permute-done((f32[64,384]{1,0:T(8,128)S(1)}, f32[64,384]{1,0:T(8,128)S(1)}, u32[]{:S(2)}, u32[]{:S(2)}) %collective-permute-start.26) | collective-permute-done | bytes 98336 | tf_op jit(solution)/shard_map/ppermute | solution.py:20
  144.3 5.3 %shard_map.56 = (f32[128,384]{1,0:T(8,128)S(1)}, f32[128,256]{1,0:T(8,128)S(1)}) custom-call(s32[1]{0:T(128)} %bitcast.index_ref, f32[64,384]{1,0:T(8,128)S(1)} %add.38.own_ref, f32[64,384]{1,0:T(8,128)S(1)} %collective-permute-done.27.got_ref), custom_call_target="tpu_custom_call" | custom-call | flops 205520896 | bytes 524288 | tf_op jit(solution)/shard_map/pallas_call | solution.py:133
  152.3 5.1 %shard_map.48.solved_ref = f32[1024,640]{1,0:T(8,128)S(1)} custom-call(f32[1024,384]{1,0:T(8,128)S(1)} %get-tuple-element.42.head_ref, f32[1024,768]{1,0:T(8,128)S(1)} %shard_map.37.x_ref.tail_ref, f32[128,1024]{1,0:T(8,128)S(1)} %get-tuple-element.44.w_ref.w0, f32[128,896]{1,0:T(8,128)S(1)} %get-tuple-element.51.w_ref.w1, ...), custom_call_target="tpu_custom_call" | custom-call | flops 2013265920 | bytes 9043968 | tf_op jit(solution)/shard_map/pallas_call | solution.py:133
  161.3 5.4 %shard_map.59 = (f32[128,256]{1,0:T(8,128)}, f32[128,128]{1,0:T(8,128)S(1)}) custom-call(s32[1]{0:T(128)} %bitcast.index_ref, f32[64,256]{1,0:T(8,128)S(1)} %add.39.own_ref, f32[64,256]{1,0:T(8,128)S(1)} %collective-permute-done.30.got_ref), custom_call_target="tpu_custom_call" | custom-call | flops 192937984 | bytes 327680 | tf_op jit(solution)/shard_map/pallas_call | solution.py:133
  (87 shorter events, 54.6 us)
Async XLA Ops:
  14.5 6.8 %collective-permute-start = (f32[128,2176]{1,0:T(8,128)S(1)}, f32[128,2176]{1,0:T(8,128)S(1)}, u32[]{:S(2)}, u32[]{:S(2)}) collective-permute-start(f32[128,2176]{1,0:T(8,128)S(1)} %get-tuple-element.43.own_ref), channel_id=1, source_target_pairs={{0,1},{1,0},{2,3},{3,2},{4,5},{5,4},{6,7},{7,6},{8,9},{9,8},{10,11... | collective-permute-start | bytes 3342344 | tf_op jit(solution)/shard_map/ppermute | solution.py:20
  14.6 12.3 %collective-permute-start.1 = (f32[64,896]{1,0:T(8,128)S(1)}, f32[64,896]{1,0:T(8,128)S(1)}, u32[]{:S(2)}, u32[]{:S(2)}) collective-permute-start(f32[64,896]{1,0:T(8,128)S(1)} %get-tuple-element.46), channel_id=1, source_target_pairs={{0,1},{1,0},{2,3},{3,2},{4,5},{5,4},{6,7},{7,6},{8,9},{9,8},{10,11... | collective-permute-start | bytes 688136 | tf_op jit(solution)/shard_map/ppermute | solution.py:20
  27.5 8.4 %collective-permute-start.2 = (f32[64,1024]{1,0:T(8,128)S(1)}, f32[64,1024]{1,0:T(8,128)S(1)}, u32[]{:S(2)}, u32[]{:S(2)}) collective-permute-start(f32[64,1024]{1,0:T(8,128)S(1)} %get-tuple-element.48), channel_id=1, source_target_pairs={{0,2},{1,3},{2,0},{3,1},{4,6},{5,7},{6,4},{7,5},{8,10},{9,11},{10,... | collective-permute-start | bytes 786440 | tf_op jit(solution)/shard_map/ppermute | solution.py:20
  30.7 16.0 %collective-permute-start.5 = (f32[64,2560]{1,0:T(8,128)S(1)}, f32[64,2560]{1,0:T(8,128)S(1)}, u32[]{:S(2)}, u32[]{:S(2)}) collective-permute-start(f32[64,2560]{1,0:T(8,128)S(1)} %get-tuple-element.55), channel_id=1, source_target_pairs={{0,1},{1,0},{2,3},{3,2},{4,5},{5,4},{6,7},{7,6},{8,9},{9,8},{10,11... | collective-permute-start | bytes 1966088 | tf_op jit(solution)/shard_map/ppermute | solution.py:20
  36.1 8.0 %collective-permute-start.4 = (f32[64,896]{1,0:T(8,128)S(1)}, f32[64,896]{1,0:T(8,128)S(1)}, u32[]{:S(2)}, u32[]{:S(2)}) collective-permute-start(f32[64,896]{1,0:T(8,128)S(1)} %get-tuple-element.52.own_ref), channel_id=1, source_target_pairs={{0,2},{1,3},{2,0},{3,1},{4,6},{5,7},{6,4},{7,5},{8,10},{9,11},{10,... | collective-permute-start | bytes 688136 | tf_op jit(solution)/shard_map/ppermute | solution.py:20
  44.5 8.5 %collective-permute-start.6 = (f32[64,896]{1,0:T(8,128)S(1)}, f32[64,896]{1,0:T(8,128)S(1)}, u32[]{:S(2)}, u32[]{:S(2)}) collective-permute-start(f32[64,896]{1,0:T(8,128)S(1)} %shard_map.41), channel_id=1, source_target_pairs={{0,4},{1,5},{2,6},{3,7},{4,0},{5,1},{6,2},{7,3},{8,12},{9,13},{10,... | collective-permute-start | bytes 688136 | tf_op jit(solution)/shard_map/ppermute | solution.py:20
  52.9 7.1 %collective-permute-start.10 = (f32[16,2560]{1,0:T(8,128)S(1)}, f32[16,2560]{1,0:T(8,128)S(1)}, u32[]{:S(2)}, u32[]{:S(2)}) collective-permute-start(f32[16,2560]{1,0:T(8,128)S(1)} %get-tuple-element.66), channel_id=1, source_target_pairs={{0,2},{1,3},{2,0},{3,1},{4,6},{5,7},{6,4},{7,5},{8,10},{9,11},{10,... | collective-permute-start | bytes 491528 | tf_op jit(solution)/shard_map/ppermute | solution.py:20
  53.4 7.9 %collective-permute-start.9 = (f32[16,2560]{1,0:T(8,128)S(1)}, f32[16,2560]{1,0:T(8,128)S(1)}, u32[]{:S(2)}, u32[]{:S(2)}) collective-permute-start(f32[16,2560]{1,0:T(8,128)S(1)} %get-tuple-element.65), channel_id=1, source_target_pairs={{0,6},{1,7},{2,4},{3,5},{4,2},{5,3},{6,0},{7,1},{8,14},{9,15},{10,... | collective-permute-start | bytes 491528 | tf_op jit(solution)/shard_map/ppermute | solution.py:20
  55.6 7.1 %collective-permute-start.8 = (f32[16,2560]{1,0:T(8,128)S(1)}, f32[16,2560]{1,0:T(8,128)S(1)}, u32[]{:S(2)}, u32[]{:S(2)}) collective-permute-start(f32[16,2560]{1,0:T(8,128)S(1)} %get-tuple-element.64), channel_id=1, source_target_pairs={{0,4},{1,5},{2,6},{3,7},{4,0},{5,1},{6,2},{7,3},{8,12},{9,13},{10,... | collective-permute-start | bytes 491528 | tf_op jit(solution)/shard_map/ppermute | solution.py:20
  57.0 5.7 %collective-permute-start.7 = (f32[64,896]{1,0:T(8,128)S(1)}, f32[64,896]{1,0:T(8,128)S(1)}, u32[]{:S(2)}, u32[]{:S(2)}) collective-permute-start(f32[64,896]{1,0:T(8,128)S(1)} %add.31.own_ref), channel_id=1, source_target_pairs={{0,1},{1,0},{2,3},{3,2},{4,5},{5,4},{6,7},{7,6},{8,9},{9,8},{10,11... | collective-permute-start | bytes 688136 | tf_op jit(solution)/shard_map/ppermute | solution.py:20
  68.9 5.4 %collective-permute-start.11 = (f32[16,2560]{1,0:T(8,128)S(1)}, f32[16,2560]{1,0:T(8,128)S(1)}, u32[]{:S(2)}, u32[]{:S(2)}) collective-permute-start(f32[16,2560]{1,0:T(8,128)S(1)} %shard_map.46), channel_id=1, source_target_pairs={{0,8},{1,9},{2,10},{3,11},{4,12},{5,13},{6,14},{7,15},{8,0},{9,1},... | collective-permute-start | bytes 491528 | tf_op jit(solution)/shard_map/ppermute | solution.py:20
  74.4 4.2 %collective-permute-start.14 = (f32[16,768]{1,0:T(8,128)S(1)}, f32[16,768]{1,0:T(8,128)S(1)}, u32[]{:S(2)}, u32[]{:S(2)}) collective-permute-start(f32[16,768]{1,0:T(8,128)S(1)} %get-tuple-element.80), channel_id=1, source_target_pairs={{0,6},{1,7},{2,4},{3,5},{4,2},{5,3},{6,0},{7,1},{8,14},{9,15},{10,... | collective-permute-start | bytes 147464 | tf_op jit(solution)/shard_map/ppermute | solution.py:20
  75.6 5.6 %collective-permute-start.13 = (f32[16,768]{1,0:T(8,128)S(1)}, f32[16,768]{1,0:T(8,128)S(1)}, u32[]{:S(2)}, u32[]{:S(2)}) collective-permute-start(f32[16,768]{1,0:T(8,128)S(1)} %get-tuple-element.80), channel_id=1, source_target_pairs={{0,4},{1,5},{2,6},{3,7},{4,0},{5,1},{6,2},{7,3},{8,12},{9,13},{10,... | collective-permute-start | bytes 147464 | tf_op jit(solution)/shard_map/ppermute | solution.py:20
  78.4 4.1 %collective-permute-start.12 = (f32[16,768]{1,0:T(8,128)S(1)}, f32[16,768]{1,0:T(8,128)S(1)}, u32[]{:S(2)}, u32[]{:S(2)}) collective-permute-start(f32[16,768]{1,0:T(8,128)S(1)} %get-tuple-element.80), channel_id=1, source_target_pairs={{0,2},{1,3},{2,0},{3,1},{4,6},{5,7},{6,4},{7,5},{8,10},{9,11},{10,... | collective-permute-start | bytes 147464 | tf_op jit(solution)/shard_map/ppermute | solution.py:20
  90.1 9.3 %collective-permute-start.16 = (f32[16,1792]{1,0:T(8,128)S(1)}, f32[16,1792]{1,0:T(8,128)S(1)}, u32[]{:S(2)}, u32[]{:S(2)}) collective-permute-start(f32[16,1792]{1,0:T(8,128)S(1)} %shard_map.49), channel_id=1, source_target_pairs={{0,16},{1,17},{2,18},{3,19},{4,20},{5,21},{6,22},{7,23},{8,24},{9,... | collective-permute-start | bytes 344072 | tf_op jit(solution)/shard_map/ppermute | solution.py:20
  99.4 4.2 %collective-permute-start.19 = (f32[16,640]{1,0:T(8,128)S(1)}, f32[16,640]{1,0:T(8,128)S(1)}, u32[]{:S(2)}, u32[]{:S(2)}) collective-permute-start(f32[16,640]{1,0:T(8,128)S(1)} %get-tuple-element.82), channel_id=1, source_target_pairs={{0,6},{1,7},{2,4},{3,5},{4,2},{5,3},{6,0},{7,1},{8,14},{9,15},{10,... | collective-permute-start | bytes 122888 | tf_op jit(solution)/shard_map/ppermute | solution.py:20
  100.5 5.5 %collective-permute-start.18 = (f32[16,640]{1,0:T(8,128)S(1)}, f32[16,640]{1,0:T(8,128)S(1)}, u32[]{:S(2)}, u32[]{:S(2)}) collective-permute-start(f32[16,640]{1,0:T(8,128)S(1)} %get-tuple-element.82), channel_id=1, source_target_pairs={{0,4},{1,5},{2,6},{3,7},{4,0},{5,1},{6,2},{7,3},{8,12},{9,13},{10,... | collective-permute-start | bytes 122888 | tf_op jit(solution)/shard_map/ppermute | solution.py:20
  114.0 9.3 %collective-permute-start.21 = (f32[16,1152]{1,0:T(8,128)S(1)}, f32[16,1152]{1,0:T(8,128)S(1)}, u32[]{:S(2)}, u32[]{:S(2)}) collective-permute-start(f32[16,1152]{1,0:T(8,128)S(1)} %shard_map.52), channel_id=1, source_target_pairs={{0,32},{1,33},{2,34},{3,35},{4,36},{5,37},{6,38},{7,39},{8,40},{9,... | collective-permute-start | bytes 221192 | tf_op jit(solution)/shard_map/ppermute | solution.py:20
  123.3 4.5 %collective-permute-start.24 = (f32[16,1152]{1,0:T(8,128)S(1)}, f32[16,1152]{1,0:T(8,128)S(1)}, u32[]{:S(2)}, u32[]{:S(2)}) collective-permute-start(f32[16,1152]{1,0:T(8,128)S(1)} %add.37), channel_id=1, source_target_pairs={{0,6},{1,7},{2,4},{3,5},{4,2},{5,3},{6,0},{7,1},{8,14},{9,15},{10,... | collective-permute-start | bytes 221192 | tf_op jit(solution)/shard_map/ppermute | solution.py:20
  124.3 5.9 %collective-permute-start.23 = (f32[16,1152]{1,0:T(8,128)S(1)}, f32[16,1152]{1,0:T(8,128)S(1)}, u32[]{:S(2)}, u32[]{:S(2)}) collective-permute-start(f32[16,1152]{1,0:T(8,128)S(1)} %add.37), channel_id=1, source_target_pairs={{0,4},{1,5},{2,6},{3,7},{4,0},{5,1},{6,2},{7,3},{8,12},{9,13},{10,... | collective-permute-start | bytes 221192 | tf_op jit(solution)/shard_map/ppermute | solution.py:20
  126.4 4.4 %collective-permute-start.22 = (f32[16,1152]{1,0:T(8,128)S(1)}, f32[16,1152]{1,0:T(8,128)S(1)}, u32[]{:S(2)}, u32[]{:S(2)}) collective-permute-start(f32[16,1152]{1,0:T(8,128)S(1)} %add.37), channel_id=1, source_target_pairs={{0,2},{1,3},{2,0},{3,1},{4,6},{5,7},{6,4},{7,5},{8,10},{9,11},{10,... | collective-permute-start | bytes 221192 | tf_op jit(solution)/shard_map/ppermute | solution.py:20
  138.0 4.9 %collective-permute-start.26 = (f32[64,384]{1,0:T(8,128)S(1)}, f32[64,384]{1,0:T(8,128)S(1)}, u32[]{:S(2)}, u32[]{:S(2)}) collective-permute-start(f32[64,384]{1,0:T(8,128)S(1)} %get-tuple-element.74), channel_id=1, source_target_pairs={{0,64},{1,65},{2,66},{3,67},{4,68},{5,69},{6,70},{7,71},{8,72},{9,... | collective-permute-start | bytes 294920 | tf_op jit(solution)/shard_map/ppermute | solution.py:20
  143.0 6.6 %collective-permute-start.28 = (f32[64,256]{1,0:T(8,128)S(1)}, f32[64,256]{1,0:T(8,128)S(1)}, u32[]{:S(2)}, u32[]{:S(2)}) collective-permute-start(f32[64,256]{1,0:T(8,128)S(1)} %get-tuple-element.76.own_ref), channel_id=1, source_target_pairs={{0,64},{1,65},{2,66},{3,67},{4,68},{5,69},{6,70},{7,71},{8,72},{9,... | collective-permute-start | bytes 196616 | tf_op jit(solution)/shard_map/ppermute | solution.py:20
  149.9 7.5 %collective-permute-start.29 = (f32[64,256]{1,0:T(8,128)S(1)}, f32[64,256]{1,0:T(8,128)S(1)}, u32[]{:S(2)}, u32[]{:S(2)}) collective-permute-start(f32[64,256]{1,0:T(8,128)S(1)} %shard_map.58), channel_id=1, source_target_pairs={{0,128},{1,129},{2,130},{3,131},{4,132},{5,133},{6,134},{7,135},{8... | collective-permute-start | bytes 196616 | tf_op jit(solution)/shard_map/ppermute | solution.py:20
  (12 other events, 40.1 us)
where the time goes:
time: 171 us; the launch traced here: 168 us
  Pallas kernels  76.4 us (45%)
  waiting for transfers between devices  48.6 us (28%)
  starting transfers between devices  37.2 us (22%)
  local copies, waits for them, and re-layouts  5.45 us (3%)
    pallas_call x24, Pallas kernels, call(): pl.pallas_call(kernel, out_shape=outs, in_specs=(smem() if head else [])...  67.4 us
    ppermute x31, waiting for transfers between devices, swap(): lax.ppermute(value, 'leaf', [(i, i ^ mask) for i in range(lax.axis_size('...  48.6 us
    ppermute x31, starting transfers between devices, swap(): lax.ppermute(value, 'leaf', [(i, i ^ mask) for i in range(lax.axis_size('...  37.2 us
    pallas_call x1, Pallas kernels, head(): pl.pallas_call(head_kernel, name='head', out_shape=(out(leaf, HEAD), out(...  9.07 us
    unnamed x10, local copies, waits for them, and re-layouts  5.42 us
  transfers between devices with their start and end apart: 31, of which 22 were waited for; matrix products, arithmetic and copies ran while one was open for 0% of the time, Pallas kernels for 21%

commit v1 on v0

--- a/solution.py
+++ b/solution.py
@@ -12,7 +12,7 @@
 LEVELS = 8
 F32 = jnp.float32
 CORE_MASK = 1
-TURNS = 8
+TURNS = 4
 RING_MASKS = (2, 4, 6)
 
 
@@ -63,50 +63,46 @@
     turns = TURNS
     per_turn = count // turns
 
+    def add_up(terms):
+        while len(terms) > 1:
+            terms = [a + b for a, b in zip(terms[::2], terms[1::2])]
+        return terms[0]
+
     def eliminate(rows, p):
-        rows = list(rows)
-        panel = rows[p]
         base = 8 * p
-        panel_rows = [spread_row(panel, j) for j in range(8)]
-        d = [spread_col(panel, base + j) for j in range(8)]
+        panel_rows = [spread_row(rows[p], j) for j in range(8)]
+        d = [spread_col(rows[p], base + j) for j in range(8)]
         for a in range(0, 8, 2):
             b = a + 1
             ra = [spread_row(d[j], a) for j in range(8)]
             rb = [spread_row(d[j], b) for j in range(8)]
             inv_det = 1.0 / (ra[a] * rb[b] - ra[b] * rb[a])
             ma, mb = sub == a, sub == b
-            ca, cb = d[a], d[b]
-            ta = (ca * rb[b] - cb * rb[a]) * inv_det
-            tb = (cb * ra[a] - ca * ra[b]) * inv_det
-            iaa, iab = rb[b] * inv_det, -(ra[b] * inv_det)
-            iba, ibb = -(rb[a] * inv_det), ra[a] * inv_det
+            va = jnp.where(ma, -rb[b], jnp.where(mb, rb[a], d[a] * rb[b] - d[b] * rb[a]))
+            vb = jnp.where(ma, ra[b], jnp.where(mb, -ra[a], d[b] * ra[a] - d[a] * ra[b]))
             for j in range(8):
                 if j == a:
-                    d[j] = jnp.where(ma, iaa, jnp.where(mb, iba, -ta))
+                    d[j] = -(va * inv_det)
                 elif j == b:
-                    d[j] = jnp.where(ma, iab, jnp.where(mb, ibb, -tb))
+                    d[j] = -(vb * inv_det)
                 else:
-                    na = iaa * ra[j] + iab * rb[j]
-                    nb = iba * ra[j] + ibb * rb[j]
-                    d[j] = jnp.where(ma, na, jnp.where(mb, nb, d[j] - (ta * ra[j] + tb * rb[j])))
+                    d[j] = jnp.where(ma | mb, 0.0, d[j]) - (va * ra[j] + vb * rb[j]) * inv_det
         inside = (lane >= base) & (lane < base + 8)
-        panel = None
-        for j in range(8):
-            term = d[j] * jnp.where(inside, jnp.where(lane == base + j, 1.0, 0.0), panel_rows[j])
-            panel = term if panel is None else panel + term
-        rows[p] = panel
-        spread = [spread_row(panel, j) for j in range(8)]
-        for step in range(1, count):
-            i = (p + step) % count
-            c = rows[i]
-            total = None
-            for j in range(0, 8, 2):
-                pair = spread_col(c, base + j) * spread[j] + spread_col(c, base + j + 1) * spread[j + 1]
-                total = pair if total is None else total + pair
-            rows[i] = jnp.where(inside, 0.0, c) - total
-        return rows
+        panel = add_up(
+            [d[j] * jnp.where(inside, jnp.where(lane == base + j, 1.0, 0.0), panel_rows[j]) for j in range(8)]
+        )
+        after = (p + 1) % count
+        ahead = add_up([spread_col(rows[after], base + j) * spread_row(panel, j) for j in range(8)])
+        ahead = jnp.where(inside, 0.0, rows[after]) - ahead
+        zeros = [jnp.zeros((8, R), F32)]
+        pivot_rows = jnp.concatenate(zeros * p + [panel] + zeros * (count - 1 - p), axis=0)
+        change = dot_split(split(jnp.concatenate(rows, axis=0)), split(pivot_rows))
+        result = [jnp.where(inside, 0.0, row) - change[8 * i : 8 * i + 8, :] for i, row in enumerate(rows)]
+        result[p], result[after] = panel, ahead
+        return result
 
     def turn(_, rows):
+        rows = list(rows)
         for p in range(per_turn):
             rows = eliminate(rows, p)
         rows = rows[per_turn:] + rows[:per_turn]
@@ -222,7 +218,7 @@
             pltpu.SemaphoreType.DMA((3,)),
         ],
         cost_estimate=pl.CostEstimate(flops=6 * leaf * R * 54 * R, bytes_accessed=8 * leaf * leaf, transcendentals=0),
-        compiler_params=pltpu.CompilerParams(vmem_limit_bytes=24 << 20),
+        compiler_params=pltpu.CompilerParams(vmem_limit_bytes=60 << 20),
     )(index, leaf_inverse, bases, white_noise)
 
 
@@ -470,7 +466,6 @@
         scratch=(pltpu.VMEM((R, width3), F32),),
         flops=update_flops(2),
     )
-    quarters, got = lax.optimization_barrier((quarters, got))
     half = half + got
     other = swap(half, CORE_MASK)
     panel, w = invert(2, half, other, index)
@@ -482,7 +477,8 @@
     for level in range(2, 6):
         width = (LEVELS + 1 - level) * R
         if level > 2:
-            rest = rest + swap(rest, 1 << level)
+            got_rest = swap(rest, 1 << level)
+            rest = rest + got_rest
             if level < 5:
                 row = ring_all(rest[:, :width])
             else:
@@ -519,12 +515,14 @@
             )
         elif level > 3:
             solved = solve_step(solved, w)
-    got, got_rest = swap(half, 64), swap(rest, 64)
+    got = swap(half, 64)
+    got_rest = swap(rest, 64)
     half = half + got
     panel, w = invert(6, half, swap(half, CORE_MASK), index)
     solved = solve_step(solved, w)
     (half,) = call(update6_kernel, (out(HALF, 2 * R),), (rest, got_rest, panel, w), index=index, flops=update_flops(6))
-    half = half + swap(half, 128)
+    got = swap(half, 128)
+    half = half + got
     _, w = invert(7, half, swap(half, CORE_MASK), index)
     return solve_step(solved, w)
 

time: 171 us -> 165 us (0.965)
  the two profiles are of different devices: /device:TPU:10 before, /device:TPU:1 now
where the time goes in v1:
time: 165 us
  Pallas kernels  69.4 us (42%)
  starting transfers between devices  49.4 us (30%)
  waiting for transfers between devices  41.2 us (25%)
  local copies, waits for them, and re-layouts  4.42 us (3%)
    pallas_call x24, Pallas kernels, call(): pl.pallas_call(kernel, out_shape=outs, in_specs=(smem() if head else [])...  57.9 us
    ppermute x31, starting transfers between devices, swap(): lax.ppermute(value, 'leaf', [(i, i ^ mask) for i in range(lax.axis_size('...  49.4 us
    ppermute x31, waiting for transfers between devices, swap(): lax.ppermute(value, 'leaf', [(i, i ^ mask) for i in range(lax.axis_size('...  41.2 us
    pallas_call x1, Pallas kernels, head(): pl.pallas_call(head_kernel, name='head', out_shape=(out(leaf, HEAD), out(...  11.5 us
    unnamed x14, local copies, waits for them, and re-layouts  4.4 us
  transfers between devices with their start and end apart: 31, of which 19 were waited for; matrix products, arithmetic and copies ran while one was open for 0% of the time, Pallas kernels for 20%

profile of v1, /device:TPU:1, one launch (start us, length us, event | category | flops | bytes accessed | tf_op | source)
XLA Modules:
  0.0 165.0 jit_solution(6844585865434769443)
XLA Ops:
  0.0 11.5 %head.1 = (f32[1024,384]{1,0:T(8,128)}, f32[128,2176]{1,0:T(8,128)}, f32[64,896]{1,0:T(8,128)}, f32[64,896]{1,0:T(8,128)}) custom-call(s32[1]{0:T(128)} %bitcast.index_ref, f32[1024,1024]{1,0:T(8,128)} %a_ref.1, f32[1024,1024]{1,0:T(8,128)} %u_ref.3, f32[1024,128]{1,0:T(8,128)} %w_ref.1), custom_call_target="tpu_custom_call" | custom-call | flops 5435817984 | bytes 8388608 | tf_op jit(solution)/shard_map/head/pallas_call | solution.py:204
  11.5 3.3 %collective-permute-start = (f32[128,2176]{1,0:T(8,128)}, f32[128,2176]{1,0:T(8,128)S(1)}, u32[]{:S(2)}, u32[]{:S(2)}) collective-permute-start(f32[128,2176]{1,0:T(8,128)} %get-tuple-element.38.own_ref), channel_id=1, source_target_pairs={{0,1},{1,0},{2,3},{3,2},{4,5},{5,4},{6,7},{7,6},{8,9},{9,8},{10,11... | collective-permute-start | bytes 3342344 | tf_op jit(solution)/shard_map/ppermute | solution.py:20
  19.2 6.1 %shard_map.37.x_ref.tail_ref = f32[1024,768]{1,0:T(8,128)S(1)} custom-call(f32[1024,1024]{1,0:T(8,128)S(1)} %copy-done.3, f32[1024,1024]{1,0:T(8,128)S(1)} %copy-done.4, f32[1024,128]{1,0:T(8,128)S(1)} %copy-done.6), custom_call_target="tpu_custom_call" | custom-call | flops 4831838208 | bytes 12058624 | tf_op jit(solution)/shard_map/pallas_call | solution.py:129
  25.4 2.5 %shard_map.43 = (f32[64,2560]{1,0:T(8,128)S(1)}, f32[64,2560]{1,0:T(8,128)S(1)}) custom-call(s32[1]{0:T(128)} %bitcast.index_ref, f32[1024,1024]{1,0:T(8,128)S(1)} %copy-done.5, f32[1024,768]{1,0:T(8,128)S(1)} %shard_map.37.x_ref.tail_ref), custom_call_target="tpu_custom_call" | custom-call | flops 2013265920 | bytes 8650752 | tf_op jit(solution)/shard_map/pallas_call | solution.py:129
  28.4 4.4 %shard_map.38 = (f32[128,1152]{1,0:T(8,128)S(1)}, f32[128,1024]{1,0:T(8,128)S(1)}) custom-call(f32[128,2176]{1,0:T(8,128)S(1)} %copy-done, f32[128,2176]{1,0:T(8,128)S(1)} %collective-permute-done.got_ref), custom_call_target="tpu_custom_call" | custom-call | flops 281018368 | bytes 3342336 | tf_op jit(solution)/shard_map/pallas_call | solution.py:129
  33.5 7.7 %collective-permute-done.2 = f32[64,1024]{1,0:T(8,128)S(1)} collective-permute-done((f32[64,1024]{1,0:T(8,128)S(1)}, f32[64,1024]{1,0:T(8,128)S(1)}, u32[]{:S(2)}, u32[]{:S(2)}) %collective-permute-start.2) | collective-permute-done | bytes 262176 | tf_op jit(solution)/shard_map/ppermute | solution.py:20
  43.5 4.4 %shard_map.40 = (f32[128,1024]{1,0:T(8,128)S(1)}, f32[128,896]{1,0:T(8,128)S(1)}) custom-call(s32[1]{0:T(128)} %bitcast.index_ref, f32[64,1024]{1,0:T(8,128)S(1)} %add.30.own_ref, f32[64,1024]{1,0:T(8,128)S(1)} %collective-permute-done.3.got_ref), custom_call_target="tpu_custom_call" | custom-call | flops 268435456 | bytes 1507328 | tf_op jit(solution)/shard_map/pallas_call | solution.py:129
  57.8 3.3 %collective-permute-start.6 = (f32[64,896]{1,0:T(8,128)S(1)}, f32[64,896]{1,0:T(8,128)S(1)}, u32[]{:S(2)}, u32[]{:S(2)}) collective-permute-start(f32[64,896]{1,0:T(8,128)S(1)} %add.31.own_ref), channel_id=1, source_target_pairs={{0,1},{1,0},{2,3},{3,2},{4,5},{5,4},{6,7},{7,6},{8,9},{9,8},{10,11... | collective-permute-start | bytes 688136 | tf_op jit(solution)/shard_map/ppermute | solution.py:20
  64.8 4.3 %shard_map.42 = (f32[128,896]{1,0:T(8,128)S(1)}, f32[128,768]{1,0:T(8,128)S(1)}) custom-call(s32[1]{0:T(128)} %bitcast.index_ref, f32[64,896]{1,0:T(8,128)S(1)} %add.31.own_ref, f32[64,896]{1,0:T(8,128)S(1)} %collective-permute-done.6.got_ref), custom_call_target="tpu_custom_call" | custom-call | flops 255852544 | bytes 1310720 | tf_op jit(solution)/shard_map/pallas_call | solution.py:129
  70.0 4.2 %collective-permute-done.11 = f32[16,2560]{1,0:T(8,128)S(1)} collective-permute-done((f32[16,2560]{1,0:T(8,128)S(1)}, f32[16,2560]{1,0:T(8,128)S(1)}, u32[]{:S(2)}, u32[]{:S(2)}) %collective-permute-start.11) | collective-permute-done | bytes 163872 | tf_op jit(solution)/shard_map/ppermute | solution.py:20
  79.7 4.5 %collective-permute-start.15 = (f32[4,16,768]{2,1,0:T(8,128)S(1)}, f32[4,16,768]{2,1,0:T(8,128)S(1)}, u32[]{:S(2)}, u32[]{:S(2)}) collective-permute-start(f32[4,16,768]{2,1,0:T(8,128)S(1)} %pad_maximum_fusion.1.own_ref), channel_id=1, source_target_pairs={{0,1},{1,0},{2,3},{3,2},{4,5},{5,4},{6,7},{7,6},{8,9},{9,8},{10,11... | collective-permute-start | bytes 589832 | tf_op jit(solution)/shard_map/ppermute | solution.py:20
  85.2 4.3 %shard_map.47 = (f32[128,768]{1,0:T(8,128)S(1)}, f32[128,640]{1,0:T(8,128)S(1)}) custom-call(s32[1]{0:T(128)} %bitcast.index_ref, f32[4,16,768]{2,1,0:T(8,128)S(1)} %pad_maximum_fusion.1.own_ref, f32[4,16,768]{2,1,0:T(8,128)S(1)} %collective-permute-done.15.got_ref), custom_call_target="tpu_custom_call" | custom-call | flops 243269632 | bytes 1114112 | tf_op jit(solution)/shard_map/pallas_call | solution.py:129
  90.1 2.9 %collective-permute-start.16 = (f32[16,1792]{1,0:T(8,128)S(1)}, f32[16,1792]{1,0:T(8,128)S(1)}, u32[]{:S(2)}, u32[]{:S(2)}) collective-permute-start(f32[16,1792]{1,0:T(8,128)S(1)} %shard_map.49), channel_id=1, source_target_pairs={{0,16},{1,17},{2,18},{3,19},{4,20},{5,21},{6,22},{7,23},{8,24},{9,... | collective-permute-start | bytes 344072 | tf_op jit(solution)/shard_map/ppermute | solution.py:20
  93.0 5.6 %collective-permute-done.16 = f32[16,1792]{1,0:T(8,128)S(1)} collective-permute-done((f32[16,1792]{1,0:T(8,128)S(1)}, f32[16,1792]{1,0:T(8,128)S(1)}, u32[]{:S(2)}, u32[]{:S(2)}) %collective-permute-start.16) | collective-permute-done | bytes 114720 | tf_op jit(solution)/shard_map/ppermute | solution.py:20
  104.1 2.9 %collective-permute-start.20 = (f32[4,16,640]{2,1,0:T(8,128)S(1)}, f32[4,16,640]{2,1,0:T(8,128)S(1)}, u32[]{:S(2)}, u32[]{:S(2)}) collective-permute-start(f32[4,16,640]{2,1,0:T(8,128)S(1)} %pad_maximum_fusion.2.own_ref), channel_id=1, source_target_pairs={{0,1},{1,0},{2,3},{3,2},{4,5},{5,4},{6,7},{7,6},{8,9},{9,8},{10,11... | collective-permute-start | bytes 491528 | tf_op jit(solution)/shard_map/ppermute | solution.py:20
  108.1 4.2 %shard_map.50 = (f32[128,640]{1,0:T(8,128)S(1)}, f32[128,512]{1,0:T(8,128)S(1)}) custom-call(s32[1]{0:T(128)} %bitcast.index_ref, f32[4,16,640]{2,1,0:T(8,128)S(1)} %pad_maximum_fusion.2.own_ref, f32[4,16,640]{2,1,0:T(8,128)S(1)} %collective-permute-done.20.got_ref), custom_call_target="tpu_custom_call" | custom-call | flops 230686720 | bytes 917504 | tf_op jit(solution)/shard_map/pallas_call | solution.py:129
  112.8 6.2 %collective-permute-start.21 = (f32[16,1152]{1,0:T(8,128)S(1)}, f32[16,1152]{1,0:T(8,128)S(1)}, u32[]{:S(2)}, u32[]{:S(2)}) collective-permute-start(f32[16,1152]{1,0:T(8,128)S(1)} %shard_map.52), channel_id=1, source_target_pairs={{0,32},{1,33},{2,34},{3,35},{4,36},{5,37},{6,38},{7,39},{8,40},{9,... | collective-permute-start | bytes 221192 | tf_op jit(solution)/shard_map/ppermute | solution.py:20
  127.8 2.4 %collective-permute-start.25 = (f32[4,16,512]{2,1,0:T(8,128)S(1)}, f32[4,16,512]{2,1,0:T(8,128)S(1)}, u32[]{:S(2)}, u32[]{:S(2)}) collective-permute-start(f32[4,16,512]{2,1,0:T(8,128)S(1)} %slice.14.own_ref), channel_id=1, source_target_pairs={{0,1},{1,0},{2,3},{3,2},{4,5},{5,4},{6,7},{7,6},{8,9},{9,8},{10,11... | collective-permute-start | bytes 393224 | tf_op jit(solution)/shard_map/ppermute | solution.py:20
  131.1 4.2 %shard_map.53 = (f32[128,512]{1,0:T(8,128)S(1)}, f32[128,384]{1,0:T(8,128)S(1)}) custom-call(s32[1]{0:T(128)} %bitcast.index_ref, f32[4,16,512]{2,1,0:T(8,128)S(1)} %slice.14.own_ref, f32[4,16,512]{2,1,0:T(8,128)S(1)} %collective-permute-done.25.got_ref), custom_call_target="tpu_custom_call" | custom-call | flops 218103808 | bytes 720896 | tf_op jit(solution)/shard_map/pallas_call | solution.py:129
  137.1 2.7 %collective-permute-done.26 = f32[64,384]{1,0:T(8,128)S(1)} collective-permute-done((f32[64,384]{1,0:T(8,128)S(1)}, f32[64,384]{1,0:T(8,128)S(1)}, u32[]{:S(2)}, u32[]{:S(2)}) %collective-permute-start.26) | collective-permute-done | bytes 98336 | tf_op jit(solution)/shard_map/ppermute | solution.py:20
  142.4 4.2 %shard_map.56 = (f32[128,384]{1,0:T(8,128)S(1)}, f32[128,256]{1,0:T(8,128)S(1)}) custom-call(s32[1]{0:T(128)} %bitcast.index_ref, f32[64,384]{1,0:T(8,128)S(1)} %add.38.own_ref, f32[64,384]{1,0:T(8,128)S(1)} %collective-permute-done.27.got_ref), custom_call_target="tpu_custom_call" | custom-call | flops 205520896 | bytes 524288 | tf_op jit(solution)/shard_map/pallas_call | solution.py:129
  146.9 2.7 %collective-permute-start.29 = (f32[64,256]{1,0:T(8,128)S(1)}, f32[64,256]{1,0:T(8,128)S(1)}, u32[]{:S(2)}, u32[]{:S(2)}) collective-permute-start(f32[64,256]{1,0:T(8,128)S(1)} %shard_map.58), channel_id=1, source_target_pairs={{0,128},{1,129},{2,130},{3,131},{4,132},{5,133},{6,134},{7,135},{8... | collective-permute-start | bytes 196616 | tf_op jit(solution)/shard_map/ppermute | solution.py:20
  149.6 5.0 %shard_map.48.solved_ref = f32[1024,640]{1,0:T(8,128)S(1)} custom-call(f32[1024,384]{1,0:T(8,128)S(1)} %copy-done.1, f32[1024,768]{1,0:T(8,128)S(1)} %shard_map.37.x_ref.tail_ref, f32[128,1024]{1,0:T(8,128)S(1)} %get-tuple-element.39.w_ref.w0, f32[128,896]{1,0:T(8,128)S(1)} %get-tuple-element.46.w_ref.w1, f32[128,768]{1,0:T(8,128)S(1)} %get-tuple-element.49.w_ref.w2, ...), custom_call_target="tpu_custom_call" | custom-call | flops 2013265920 | bytes 9043968 | tf_op jit(solution)/shard_map/pallas_call | solution.py:129
  159.2 4.2 %shard_map.59 = (f32[128,256]{1,0:T(8,128)}, f32[128,128]{1,0:T(8,128)S(1)}) custom-call(s32[1]{0:T(128)} %bitcast.index_ref, f32[64,256]{1,0:T(8,128)S(1)} %add.39.own_ref, f32[64,256]{1,0:T(8,128)S(1)} %collective-permute-done.30.got_ref), custom_call_target="tpu_custom_call" | custom-call | flops 192937984 | bytes 327680 | tf_op jit(solution)/shard_map/pallas_call | solution.py:129
  (91 shorter events, 56.9 us)
Async XLA Ops:
  11.5 16.9 %collective-permute-start = (f32[128,2176]{1,0:T(8,128)}, f32[128,2176]{1,0:T(8,128)S(1)}, u32[]{:S(2)}, u32[]{:S(2)}) collective-permute-start(f32[128,2176]{1,0:T(8,128)} %get-tuple-element.38.own_ref), channel_id=1, source_target_pairs={{0,1},{1,0},{2,3},{3,2},{4,5},{5,4},{6,7},{7,6},{8,9},{9,8},{10,11... | collective-permute-start | bytes 3342344 | tf_op jit(solution)/shard_map/ppermute | solution.py:20
  14.8 18.1 %collective-permute-start.1 = (f32[64,896]{1,0:T(8,128)}, f32[64,896]{1,0:T(8,128)S(1)}, u32[]{:S(2)}, u32[]{:S(2)}) collective-permute-start(f32[64,896]{1,0:T(8,128)} %get-tuple-element.41), channel_id=1, source_target_pairs={{0,1},{1,0},{2,3},{3,2},{4,5},{5,4},{6,7},{7,6},{8,9},{9,8},{10,11... | collective-permute-start | bytes 688136 | tf_op jit(solution)/shard_map/ppermute | solution.py:20
  27.9 23.2 %collective-permute-start.7 = (f32[64,2560]{1,0:T(8,128)S(1)}, f32[64,2560]{1,0:T(8,128)S(1)}, u32[]{:S(2)}, u32[]{:S(2)}) collective-permute-start(f32[64,2560]{1,0:T(8,128)S(1)} %get-tuple-element.51), channel_id=1, source_target_pairs={{0,1},{1,0},{2,3},{3,2},{4,5},{5,4},{6,7},{7,6},{8,9},{9,8},{10,11... | collective-permute-start | bytes 1966088 | tf_op jit(solution)/shard_map/ppermute | solution.py:20
  33.4 7.8 %collective-permute-start.2 = (f32[64,1024]{1,0:T(8,128)S(1)}, f32[64,1024]{1,0:T(8,128)S(1)}, u32[]{:S(2)}, u32[]{:S(2)}) collective-permute-start(f32[64,1024]{1,0:T(8,128)S(1)} %get-tuple-element.43), channel_id=1, source_target_pairs={{0,2},{1,3},{2,0},{3,1},{4,6},{5,7},{6,4},{7,5},{8,10},{9,11},{10,... | collective-permute-start | bytes 786440 | tf_op jit(solution)/shard_map/ppermute | solution.py:20
  42.4 7.1 %collective-permute-start.4 = (f32[64,896]{1,0:T(8,128)S(1)}, f32[64,896]{1,0:T(8,128)S(1)}, u32[]{:S(2)}, u32[]{:S(2)}) collective-permute-start(f32[64,896]{1,0:T(8,128)S(1)} %get-tuple-element.47.own_ref), channel_id=1, source_target_pairs={{0,2},{1,3},{2,0},{3,1},{4,6},{5,7},{6,4},{7,5},{8,10},{9,11},{10,... | collective-permute-start | bytes 688136 | tf_op jit(solution)/shard_map/ppermute | solution.py:20
  49.8 8.0 %collective-permute-start.5 = (f32[64,896]{1,0:T(8,128)S(1)}, f32[64,896]{1,0:T(8,128)S(1)}, u32[]{:S(2)}, u32[]{:S(2)}) collective-permute-start(f32[64,896]{1,0:T(8,128)S(1)} %shard_map.41), channel_id=1, source_target_pairs={{0,4},{1,5},{2,6},{3,7},{4,0},{5,1},{6,2},{7,3},{8,12},{9,13},{10,... | collective-permute-start | bytes 688136 | tf_op jit(solution)/shard_map/ppermute | solution.py:20
  52.6 8.5 %collective-permute-start.10 = (f32[16,2560]{1,0:T(8,128)S(1)}, f32[16,2560]{1,0:T(8,128)S(1)}, u32[]{:S(2)}, u32[]{:S(2)}) collective-permute-start(f32[16,2560]{1,0:T(8,128)S(1)} %get-tuple-element.56), channel_id=1, source_target_pairs={{0,2},{1,3},{2,0},{3,1},{4,6},{5,7},{6,4},{7,5},{8,10},{9,11},{10,... | collective-permute-start | bytes 491528 | tf_op jit(solution)/shard_map/ppermute | solution.py:20
  53.0 10.0 %collective-permute-start.9 = (f32[16,2560]{1,0:T(8,128)S(1)}, f32[16,2560]{1,0:T(8,128)S(1)}, u32[]{:S(2)}, u32[]{:S(2)}) collective-permute-start(f32[16,2560]{1,0:T(8,128)S(1)} %get-tuple-element.55), channel_id=1, source_target_pairs={{0,6},{1,7},{2,4},{3,5},{4,2},{5,3},{6,0},{7,1},{8,14},{9,15},{10,... | collective-permute-start | bytes 491528 | tf_op jit(solution)/shard_map/ppermute | solution.py:20
  54.9 9.9 %collective-permute-start.8 = (f32[16,2560]{1,0:T(8,128)S(1)}, f32[16,2560]{1,0:T(8,128)S(1)}, u32[]{:S(2)}, u32[]{:S(2)}) collective-permute-start(f32[16,2560]{1,0:T(8,128)S(1)} %get-tuple-element.54), channel_id=1, source_target_pairs={{0,4},{1,5},{2,6},{3,7},{4,0},{5,1},{6,2},{7,3},{8,12},{9,13},{10,... | collective-permute-start | bytes 491528 | tf_op jit(solution)/shard_map/ppermute | solution.py:20
  57.8 7.0 %collective-permute-start.6 = (f32[64,896]{1,0:T(8,128)S(1)}, f32[64,896]{1,0:T(8,128)S(1)}, u32[]{:S(2)}, u32[]{:S(2)}) collective-permute-start(f32[64,896]{1,0:T(8,128)S(1)} %add.31.own_ref), channel_id=1, source_target_pairs={{0,1},{1,0},{2,3},{3,2},{4,5},{5,4},{6,7},{7,6},{8,9},{9,8},{10,11... | collective-permute-start | bytes 688136 | tf_op jit(solution)/shard_map/ppermute | solution.py:20
  69.9 4.3 %collective-permute-start.11 = (f32[16,2560]{1,0:T(8,128)S(1)}, f32[16,2560]{1,0:T(8,128)S(1)}, u32[]{:S(2)}, u32[]{:S(2)}) collective-permute-start(f32[16,2560]{1,0:T(8,128)S(1)} %shard_map.46), channel_id=1, source_target_pairs={{0,8},{1,9},{2,10},{3,11},{4,12},{5,13},{6,14},{7,15},{8,0},{9,1},... | collective-permute-start | bytes 491528 | tf_op jit(solution)/shard_map/ppermute | solution.py:20
  74.2 4.2 %collective-permute-start.14 = (f32[16,768]{1,0:T(8,128)S(1)}, f32[16,768]{1,0:T(8,128)S(1)}, u32[]{:S(2)}, u32[]{:S(2)}) collective-permute-start(f32[16,768]{1,0:T(8,128)S(1)} %get-tuple-element.70), channel_id=1, source_target_pairs={{0,6},{1,7},{2,4},{3,5},{4,2},{5,3},{6,0},{7,1},{8,14},{9,15},{10,... | collective-permute-start | bytes 147464 | tf_op jit(solution)/shard_map/ppermute | solution.py:20
  75.2 4.4 %collective-permute-start.13 = (f32[16,768]{1,0:T(8,128)S(1)}, f32[16,768]{1,0:T(8,128)S(1)}, u32[]{:S(2)}, u32[]{:S(2)}) collective-permute-start(f32[16,768]{1,0:T(8,128)S(1)} %get-tuple-element.70), channel_id=1, source_target_pairs={{0,4},{1,5},{2,6},{3,7},{4,0},{5,1},{6,2},{7,3},{8,12},{9,13},{10,... | collective-permute-start | bytes 147464 | tf_op jit(solution)/shard_map/ppermute | solution.py:20
  79.7 5.5 %collective-permute-start.15 = (f32[4,16,768]{2,1,0:T(8,128)S(1)}, f32[4,16,768]{2,1,0:T(8,128)S(1)}, u32[]{:S(2)}, u32[]{:S(2)}) collective-permute-start(f32[4,16,768]{2,1,0:T(8,128)S(1)} %pad_maximum_fusion.1.own_ref), channel_id=1, source_target_pairs={{0,1},{1,0},{2,3},{3,2},{4,5},{5,4},{6,7},{7,6},{8,9},{9,8},{10,11... | collective-permute-start | bytes 589832 | tf_op jit(solution)/shard_map/ppermute | solution.py:20
  90.1 8.5 %collective-permute-start.16 = (f32[16,1792]{1,0:T(8,128)S(1)}, f32[16,1792]{1,0:T(8,128)S(1)}, u32[]{:S(2)}, u32[]{:S(2)}) collective-permute-start(f32[16,1792]{1,0:T(8,128)S(1)} %shard_map.49), channel_id=1, source_target_pairs={{0,16},{1,17},{2,18},{3,19},{4,20},{5,21},{6,22},{7,23},{8,24},{9,... | collective-permute-start | bytes 344072 | tf_op jit(solution)/shard_map/ppermute | solution.py:20
  98.6 4.2 %collective-permute-start.19 = (f32[16,640]{1,0:T(8,128)S(1)}, f32[16,640]{1,0:T(8,128)S(1)}, u32[]{:S(2)}, u32[]{:S(2)}) collective-permute-start(f32[16,640]{1,0:T(8,128)S(1)} %get-tuple-element.72), channel_id=1, source_target_pairs={{0,6},{1,7},{2,4},{3,5},{4,2},{5,3},{6,0},{7,1},{8,14},{9,15},{10,... | collective-permute-start | bytes 122888 | tf_op jit(solution)/shard_map/ppermute | solution.py:20
  99.7 4.4 %collective-permute-start.18 = (f32[16,640]{1,0:T(8,128)S(1)}, f32[16,640]{1,0:T(8,128)S(1)}, u32[]{:S(2)}, u32[]{:S(2)}) collective-permute-start(f32[16,640]{1,0:T(8,128)S(1)} %get-tuple-element.72), channel_id=1, source_target_pairs={{0,4},{1,5},{2,6},{3,7},{4,0},{5,1},{6,2},{7,3},{8,12},{9,13},{10,... | collective-permute-start | bytes 122888 | tf_op jit(solution)/shard_map/ppermute | solution.py:20
  112.8 8.5 %collective-permute-start.21 = (f32[16,1152]{1,0:T(8,128)S(1)}, f32[16,1152]{1,0:T(8,128)S(1)}, u32[]{:S(2)}, u32[]{:S(2)}) collective-permute-start(f32[16,1152]{1,0:T(8,128)S(1)} %shard_map.52), channel_id=1, source_target_pairs={{0,32},{1,33},{2,34},{3,35},{4,36},{5,37},{6,38},{7,39},{8,40},{9,... | collective-permute-start | bytes 221192 | tf_op jit(solution)/shard_map/ppermute | solution.py:20
  121.3 4.5 %collective-permute-start.24 = (f32[16,1152]{1,0:T(8,128)S(1)}, f32[16,1152]{1,0:T(8,128)S(1)}, u32[]{:S(2)}, u32[]{:S(2)}) collective-permute-start(f32[16,1152]{1,0:T(8,128)S(1)} %add.37), channel_id=1, source_target_pairs={{0,6},{1,7},{2,4},{3,5},{4,2},{5,3},{6,0},{7,1},{8,14},{9,15},{10,... | collective-permute-start | bytes 221192 | tf_op jit(solution)/shard_map/ppermute | solution.py:20
  122.9 4.8 %collective-permute-start.23 = (f32[16,1152]{1,0:T(8,128)S(1)}, f32[16,1152]{1,0:T(8,128)S(1)}, u32[]{:S(2)}, u32[]{:S(2)}) collective-permute-start(f32[16,1152]{1,0:T(8,128)S(1)} %add.37), channel_id=1, source_target_pairs={{0,4},{1,5},{2,6},{3,7},{4,0},{5,1},{6,2},{7,3},{8,12},{9,13},{10,... | collective-permute-start | bytes 221192 | tf_op jit(solution)/shard_map/ppermute | solution.py:20
  135.7 4.1 %collective-permute-start.26 = (f32[64,384]{1,0:T(8,128)S(1)}, f32[64,384]{1,0:T(8,128)S(1)}, u32[]{:S(2)}, u32[]{:S(2)}) collective-permute-start(f32[64,384]{1,0:T(8,128)S(1)} %get-tuple-element.64), channel_id=1, source_target_pairs={{0,64},{1,65},{2,66},{3,67},{4,68},{5,69},{6,70},{7,71},{8,72},{9,... | collective-permute-start | bytes 294920 | tf_op jit(solution)/shard_map/ppermute | solution.py:20
  141.1 5.5 %collective-permute-start.28 = (f32[64,256]{1,0:T(8,128)S(1)}, f32[64,256]{1,0:T(8,128)S(1)}, u32[]{:S(2)}, u32[]{:S(2)}) collective-permute-start(f32[64,256]{1,0:T(8,128)S(1)} %get-tuple-element.66.own_ref), channel_id=1, source_target_pairs={{0,64},{1,65},{2,66},{3,67},{4,68},{5,69},{6,70},{7,71},{8,72},{9,... | collective-permute-start | bytes 196616 | tf_op jit(solution)/shard_map/ppermute | solution.py:20
  146.9 7.8 %collective-permute-start.29 = (f32[64,256]{1,0:T(8,128)S(1)}, f32[64,256]{1,0:T(8,128)S(1)}, u32[]{:S(2)}, u32[]{:S(2)}) collective-permute-start(f32[64,256]{1,0:T(8,128)S(1)} %shard_map.58), channel_id=1, source_target_pairs={{0,128},{1,129},{2,130},{3,131},{4,132},{5,133},{6,134},{7,135},{8... | collective-permute-start | bytes 196616 | tf_op jit(solution)/shard_map/ppermute | solution.py:20
  154.6 4.5 %collective-permute-start.30 = (f32[64,256]{1,0:T(8,128)S(1)}, f32[64,256]{1,0:T(8,128)S(1)}, u32[]{:S(2)}, u32[]{:S(2)}) collective-permute-start(f32[64,256]{1,0:T(8,128)S(1)} %add.39.own_ref), channel_id=1, source_target_pairs={{0,1},{1,0},{2,3},{3,2},{4,5},{5,4},{6,7},{7,6},{8,9},{9,8},{10,11... | collective-permute-start | bytes 196616 | tf_op jit(solution)/shard_map/ppermute | solution.py:20
  (14 other events, 92.7 us)

commit v2 on v1

--- a/solution.py
+++ b/solution.py
@@ -137,18 +137,20 @@
     )(*head, *args)
 
 
-HEAD = 3 * R
 CHUNK = 256
 
 
-def head_kernel(
-    index_ref, a_hbm, u_hbm, w_hbm, x_ref, rows_ref, keep_ref, send_ref, a, u, w, u_high, u_low, row2, a_sem, sem
-):
-    core = index_ref[0] & 1
+def chunk_span(r):
+    return pl.ds(pl.multiple_of(r * CHUNK, CHUNK), CHUNK)
+
+
+def stream(lo, hi, hbm, vmem_refs, sems, split_refs, use):
+    (a_hbm, u_hbm, w_hbm), (a, u, w), (a_sem, sem) = hbm, vmem_refs, sems
+    high, low = split_refs
     chunks = a.shape[0]
     copies = [
-        pltpu.make_async_copy(u_hbm.at[:, :HEAD], u.at[:, :HEAD], sem.at[0]),
-        pltpu.make_async_copy(u_hbm.at[:, HEAD:], u.at[:, HEAD:], sem.at[1]),
+        pltpu.make_async_copy(u_hbm.at[:, lo:hi], u.at[:, lo:hi], sem.at[0]),
+        pltpu.make_async_copy(u_hbm.at[:, hi:], u.at[:, hi:], sem.at[1]),
         pltpu.make_async_copy(w_hbm, w, sem.at[2]),
     ]
 
@@ -162,64 +164,77 @@
     for r in range(1, chunks):
         a_copy(r).start()
     copies[0].wait()
-    u_high[...], u_low[...] = split(u[:, :HEAD])
-    rows_ref[...] = jnp.zeros_like(rows_ref)
-    row2[...] = jnp.zeros_like(row2)
+    high[...], low[...] = split(u[:, lo:hi])
 
     @pl.loop(0, chunks)
     def _(r):
         a_copy(r).wait()
-        span = pl.ds(pl.multiple_of(r * CHUNK, CHUNK), CHUNK)
-        x = dot_split(split(a[r]), (u_high[...], u_low[...]))
-        x_ref[span, :] = x
+        x = dot_split(split(a[r]), (high[...], low[...]))
 
         @pl.when(r == 0)
         def _():
             copies[1].wait()
             copies[2].wait()
 
+        use(chunk_span(r), x)
+
+
+def row0_kernel(a_hbm, u_hbm, w_hbm, x_ref, row_ref, a, u, w, high, low, a_sem, sem):
+    row_ref[...] = jnp.zeros_like(row_ref)
+
+    def use(span, x):
+        x_ref[span, :] = x
         x = split(x)
-        chunk_u, chunk_w = split(u[span, :]), split(w[span, :])
-        at = 0
-        for m in range(3):
-            left = cols(x, m * R, (m + 1) * R)
-            width = (LEVELS - m) * R
-            piece = dot_split(left, cols(chunk_u, m * R, LEVELS * R), (0, 0))
-            noise = dot_split(left, chunk_w, (0, 0))
-            if m < 2:
-                rows_ref[:, at : at + width] += piece
-                rows_ref[:, at + width : at + width + R] += noise
-                at += width + R
-            else:
-                row2[:, :width] += piece
-                row2[:, width:] += noise
-
-    keep_ref[...] = jnp.where(core == 0, row2[:HALF, :], row2[HALF:, :])
-    send_ref[...] = jnp.where(core == 0, row2[HALF:, :], row2[:HALF, :])
-
-
-def head(index, leaf_inverse, bases, white_noise):
-    leaf = leaf_inverse.shape[0]
-    n2 = (LEVELS - 1) * R
+        row_ref[:, : LEVELS * R] += dot_split(x, split(u[span, :]), (0, 0))
+        row_ref[:, LEVELS * R :] += dot_split(x, split(w[span, :]), (0, 0))
+
+    stream(0, R, (a_hbm, u_hbm, w_hbm), (a, u, w), (a_sem, sem), (high, low), use)
+
+
+def rows12_kernel(
+    index_ref, a_hbm, u_hbm, w_hbm, x_ref, pack_ref, keep_ref, total, a, u, w, high, low, a_sem, sem
+):
+    core = index_ref[0] & 1
+    last = (LEVELS - 1) * R
+    total[...] = jnp.zeros_like(total)
+
+    def use(span, x):
+        x_ref[span, :] = x
+        x = split(x)
+        total[:, :last] += dot_split(x, split(u[span, R:]), (0, 0))
+        total[:, last:] += dot_split(x, split(w[span, :]), (0, 0))
+
+    stream(R, 3 * R, (a_hbm, u_hbm, w_hbm), (a, u, w), (a_sem, sem), (high, low), use)
+    pack_ref[:R, :] = total[:R, :]
+    first, second = total[R : R + HALF, R:], total[R + HALF :, R:]
+    keep_ref[...] = jnp.where(core == 0, first, second)
+    pack_ref[R:, :last] = jnp.where(core == 0, second, first)
+    pack_ref[R:, last:] = jnp.zeros((HALF, R), F32)
+
+
+def stream_call(kernel, outs, args, width, grant, index=None, scratch=()):
+    leaf = args[0].shape[0]
+    head_args = () if index is None else (index,)
     return pl.pallas_call(
-        head_kernel,
-        name="head",
-        out_shape=(out(leaf, HEAD), out(R, 17 * R), out(HALF, n2), out(HALF, n2)),
-        in_specs=smem() + [pl.BlockSpec(memory_space=pltpu.HBM)] * 3,
-        out_specs=vmem(4),
+        kernel,
+        out_shape=outs,
+        in_specs=(smem() if head_args else []) + [pl.BlockSpec(memory_space=pltpu.HBM)] * 3,
+        out_specs=vmem(len(outs)),
         scratch_shapes=[
+            *scratch,
             pltpu.VMEM((leaf // CHUNK, CHUNK, leaf), F32),
             pltpu.VMEM((leaf, LEVELS * R), F32),
             pltpu.VMEM((leaf, R), F32),
-            pltpu.VMEM((leaf, HEAD), jnp.bfloat16),
-            pltpu.VMEM((leaf, HEAD), jnp.bfloat16),
-            pltpu.VMEM((R, n2), F32),
+            pltpu.VMEM((leaf, width), jnp.bfloat16),
+            pltpu.VMEM((leaf, width), jnp.bfloat16),
             pltpu.SemaphoreType.DMA((leaf // CHUNK,)),
             pltpu.SemaphoreType.DMA((3,)),
         ],
-        cost_estimate=pl.CostEstimate(flops=6 * leaf * R * 54 * R, bytes_accessed=8 * leaf * leaf, transcendentals=0),
-        compiler_params=pltpu.CompilerParams(vmem_limit_bytes=60 << 20),
-    )(index, leaf_inverse, bases, white_noise)
+        cost_estimate=pl.CostEstimate(
+            flops=6 * leaf * 17 * R * width, bytes_accessed=8 * leaf * leaf, transcendentals=0
+        ),
+        compiler_params=pltpu.CompilerParams(vmem_limit_bytes=grant << 20),
+    )(*head_args, *args)
 
 
 def tail_solve_kernel(a_ref, u_ref, w_ref, x_ref, high_ref, low_ref):
@@ -233,14 +248,20 @@
         x_ref[rows, :] = dot_split(split(a_ref[rows, :]), (high_ref[...], low_ref[...]))
 
 
-def rest_rows_kernel(index_ref, u_ref, x_ref, keep_ref, send_ref):
-    core = index_ref[0] & 1
-    x = split(x_ref[...])
-    for m, at, width in row_blocks(3)[0]:
-        u = split(u_ref[:, m * R : (m + 1) * R])
-        piece = dot_split(u, cols(x, (m - 3) * R, (LEVELS - 2) * R), (0, 0))
-        keep_ref[:, at : at + width] = jnp.where(core == 0, piece[:HALF], piece[HALF:])
-        send_ref[:, at : at + width] = jnp.where(core == 0, piece[HALF:], piece[:HALF])
+def rest_rows_kernel(index_ref, u_ref, x_ref, keep_ref, send_ref, total):
+    core = index_ref[0] & 1
+    total[...] = jnp.zeros_like(total)
+
+    @pl.loop(0, u_ref.shape[0] // CHUNK)
+    def _(r):
+        span = chunk_span(r)
+        x = split(x_ref[span, :])
+        for m, at, width in row_blocks(3)[0]:
+            u = split(u_ref[span, m * R : (m + 1) * R])
+            total[:, at : at + width] += dot_split(u, cols(x, (m - 3) * R, (LEVELS - 2) * R), (0, 0))
+
+    keep_ref[...] = jnp.where(core == 0, total[:HALF, :], total[HALF:, :])
+    send_ref[...] = jnp.where(core == 0, total[HALF:, :], total[:HALF, :])
 
 
 def invert_store(panel_ref, w_ref):
@@ -253,8 +274,7 @@
 
 
 def invert_sum_kernel(own_ref, got_ref, panel_ref, w_ref):
-    n = panel_ref.shape[1]
-    panel_ref[...] = own_ref[:, :n] + got_ref[:, :n]
+    panel_ref[...] = own_ref[...] + got_ref[...]
     invert_store(panel_ref, w_ref)
 
 
@@ -288,14 +308,15 @@
     return call(kernel, outs, (own, got), index=index, flops=flops)
 
 
-def row1_kernel(index_ref, own_ref, got_ref, keep_ref, got2_ref, panel_ref, w_ref, row_ref, half_ref, half2_ref):
+def row1_kernel(index_ref, own_ref, got_ref, keep_ref, panel_ref, w_ref, row_ref, half_ref, half2_ref):
     core = index_ref[0] & 1
     w = split(w_ref[...])
-    row = own_ref[:, 9 * R :] + got_ref[:, 9 * R :] - dot_split(split(panel_ref[:, R : 2 * R]), w, (0, 0))
+    row = own_ref[:R, :] + got_ref[:R, :] - dot_split(split(panel_ref[:, R : 2 * R]), w, (0, 0))
     row_ref[...] = row
     half_ref[...] = jnp.where(core == 0, row[:HALF], row[HALF:])
     change = dot_split(split(panel_ref[:, 2 * R : 3 * R]), cols(w, R, LEVELS * R), (0, 0))
-    half2_ref[...] = keep_ref[...] + got2_ref[...] - jnp.where(core == 0, change[:HALF], change[HALF:])
+    change = jnp.where(core == 0, change[:HALF], change[HALF:])
+    half2_ref[...] = keep_ref[...] + got_ref[R:, : (LEVELS - 1) * R] - change
 
 
 def ahead_kernel(index_ref, own_ref, got_ref, panel_ref, w_ref, half_ref):
@@ -377,6 +398,11 @@
         row_ref[...] = own_ref[...] + got_ref[...] - change
 
 
+def last_kernel(solved_ref, w_ref, solution_ref):
+    first = dot_split(split(solved_ref[:, :R]), split(w_ref[...]))
+    solution_ref[...] = solved_ref[:, R:] - first
+
+
 def solve_step_kernel(solved_ref, w_ref, next_ref):
     w = split(w_ref[...])
 
@@ -392,7 +418,7 @@
     return result
 
 
-def solve_four_kernel(head_ref, tail_ref, w0, w1, w2, w3, next_ref, high, low):
+def solve_four_kernel(x0_ref, x12_ref, tail_ref, w0, w1, w2, w3, next_ref, high, low):
     for j, w in ((3, w3), (2, w2), (1, w1), (0, w0)):
         mid = (3 - j) * R
         t = w[:, mid:]
@@ -401,11 +427,11 @@
             t = t - dot_split(split(w[:, :mid]), (high[below, :], low[below, :]))
         high[j * R : (j + 1) * R, :], low[j * R : (j + 1) * R, :] = split(t)
 
-    @pl.loop(0, head_ref.shape[0] // CHUNK)
+    @pl.loop(0, x0_ref.shape[0] // CHUNK)
     def _(r):
         span = pl.ds(pl.multiple_of(r * CHUNK, CHUNK), CHUNK)
-        change = dot_split(split(head_ref[span, :]), (high[:HEAD, :], low[:HEAD, :]))
-        change = change + dot_split(split(tail_ref[span, :R]), (high[HEAD:, :], low[HEAD:, :]))
+        x = jnp.concatenate([x0_ref[span, :], x12_ref[span, :], tail_ref[span, :R]], axis=1)
+        change = dot_split(split(x), (high[...], low[...]))
         next_ref[span, :] = tail_ref[span, R:] - change
 
 
@@ -420,16 +446,26 @@
 def tree_solve(white_noise, leaf_inverse, bases):
     index = lax.axis_index("leaf").astype(jnp.int32).reshape(1)
     leaf = leaf_inverse.shape[0]
-    x_head, rows01, keep2, send2 = head(index, leaf_inverse, bases, white_noise)
-    got01 = swap(rows01, CORE_MASK)
-    got2 = swap(send2, CORE_MASK)
+    leaf_args = (leaf_inverse, bases, white_noise)
+    x0, row0 = stream_call(row0_kernel, (out(leaf, R), out(R, 9 * R)), leaf_args, R, 56)
+    got0 = swap(row0, CORE_MASK)
+    x12, pack, keep2 = stream_call(
+        rows12_kernel,
+        (out(leaf, 2 * R), out(R + HALF, 8 * R), out(HALF, 7 * R)),
+        leaf_args,
+        2 * R,
+        50,
+        index=index,
+        scratch=(pltpu.VMEM((2 * R, 8 * R), F32),),
+    )
+    got12 = swap(pack, CORE_MASK)
     weights = []
-    panel, w = invert(0, rows01, got01, index)
+    panel, w = invert(0, row0, got0, index)
     weights.append(w)
     row1, half, half2 = call(
         row1_kernel,
         (out(R, 8 * R), out(HALF, 8 * R), out(HALF, 7 * R)),
-        (rows01, got01, keep2, got2, panel, w),
+        (pack, got12, keep2, panel, w),
         index=index,
         flops=90 * R**3,
     )
@@ -447,6 +483,7 @@
         (out(HALF, width3), out(HALF, width3)),
         (bases, x_tail),
         index=index,
+        scratch=(pltpu.VMEM((R, width3), F32),),
         flops=6 * leaf * R * width3,
     )
     got_rest = swap(send, CORE_MASK)
@@ -509,7 +546,7 @@
             (solved,) = call(
                 solve_four_kernel,
                 (out(leaf, 5 * R),),
-                (x_head, x_tail, *weights),
+                (x0, x12, x_tail, *weights),
                 scratch=(pltpu.VMEM((4 * R, 5 * R), jnp.bfloat16),) * 2,
                 flops=6 * leaf * 4 * R * 5 * R,
             )
@@ -524,7 +561,8 @@
     got = swap(half, 128)
     half = half + got
     _, w = invert(7, half, swap(half, CORE_MASK), index)
-    return solve_step(solved, w)
+    (answer,) = call(last_kernel, (out(leaf, R),), (solved, w), flops=6 * leaf * R * R)
+    return answer
 
 
 def solution(mesh):

time: 165 us -> 172 us (1.042)
  Pallas kernels: 69.4 us -> 75.1 us
  waiting for transfers between devices: 41.2 us -> 45.2 us
    pallas_call x1 -> x2, Pallas kernels: 11.5 us -> 17.6 us  [stream_call(): pl.pallas_call(kernel, out_shape=outs, in_specs=(smem() if head_args else...]
    ppermute x31, waiting for transfers between devices: 41.2 us -> 45.2 us  [swap(): lax.ppermute(value, 'leaf', [(i, i ^ mask) for i in range(lax.axis_size('...]
    unnamed x14 -> x12, local copies, waits for them, and re-layouts: 4.4 us -> 3.25 us
  transfers between devices with their start and end apart: 31 -> 31, of which waited for: 19 -> 20; matrix products, arithmetic and copies ran while one was open for 0% -> 0% of each run, Pallas kernels for 20% -> 24%
where the time goes in v2:
time: 172 us
  Pallas kernels  75.1 us (44%)
  starting transfers between devices  47.8 us (28%)
  waiting for transfers between devices  45.2 us (26%)
  local copies, waits for them, and re-layouts  3.28 us (2%)
    pallas_call x24, Pallas kernels, call(): pl.pallas_call(kernel, out_shape=outs, in_specs=(smem() if head else [])...  57.5 us
    ppermute x31, starting transfers between devices, swap(): lax.ppermute(value, 'leaf', [(i, i ^ mask) for i in range(lax.axis_size('...  47.8 us
    ppermute x31, waiting for transfers between devices, swap(): lax.ppermute(value, 'leaf', [(i, i ^ mask) for i in range(lax.axis_size('...  45.2 us
    pallas_call x2, Pallas kernels, stream_call(): pl.pallas_call(kernel, out_shape=outs, in_specs=(smem() if head_args else...  17.6 us
  transfers between devices with their start and end apart: 31, of which 20 were waited for; matrix products, arithmetic and copies ran while one was open for 0% of the time, Pallas kernels for 24%

profile of v2, /device:TPU:1, one launch (start us, length us, event | category | flops | bytes accessed | tf_op | source)
XLA Modules:
  0.0 171.9 jit_solution(7104212881315537007)
XLA Ops:
  1.0 9.8 %shard_map.38 = (f32[1024,256]{1,0:T(8,128)S(1)}, f32[192,1024]{1,0:T(8,128)S(1)}, f32[64,896]{1,0:T(8,128)S(1)}) custom-call(s32[1]{0:T(128)} %bitcast.index_ref, f32[1024,1024]{1,0:T(8,128)} %a_ref.1, f32[1024,1024]{1,0:T(8,128)} %u_ref.3, f32[1024,128]{1,0:T(8,128)S(1)} %copy-done.3), custom_call_target="tpu_custom_call" | custom-call | flops 3422552064 | bytes 8388608 | tf_op jit(solution)/shard_map/pallas_call | solution.py:218
  10.9 3.3 %collective-permute-start.1 = (f32[192,1024]{1,0:T(8,128)S(1)}, f32[192,1024]{1,0:T(8,128)S(1)}, u32[]{:S(2)}, u32[]{:S(2)}) collective-permute-start(f32[192,1024]{1,0:T(8,128)S(1)} %get-tuple-element.42.own_ref), channel_id=1, source_target_pairs={{0,1},{1,0},{2,3},{3,2},{4,5},{5,4},{6,7},{7,6},{8,9},{9,8},{10,11... | collective-permute-start | bytes 2359304 | tf_op jit(solution)/shard_map/ppermute | solution.py:20
  14.1 7.8 %shard_map.37 = (f32[1024,128]{1,0:T(8,128)}, f32[128,1152]{1,0:T(8,128)}) custom-call(f32[1024,1024]{1,0:T(8,128)} %a_ref.1, f32[1024,1024]{1,0:T(8,128)} %u_ref.3, f32[1024,128]{1,0:T(8,128)} %w_ref.1), custom_call_target="tpu_custom_call" | custom-call | flops 1711276032 | bytes 8388608 | tf_op jit(solution)/shard_map/pallas_call | solution.py:218
  24.3 6.1 %shard_map.39.x_ref.tail_ref = f32[1024,768]{1,0:T(8,128)S(1)} custom-call(f32[1024,1024]{1,0:T(8,128)S(1)} %copy-done, f32[1024,1024]{1,0:T(8,128)S(1)} %copy-done.1, f32[1024,128]{1,0:T(8,128)S(1)} %copy-done.4), custom_call_target="tpu_custom_call" | custom-call | flops 4831838208 | bytes 12058624 | tf_op jit(solution)/shard_map/pallas_call | solution.py:129
  30.5 3.3 %shard_map.45 = (f32[64,2560]{1,0:T(8,128)S(1)}, f32[64,2560]{1,0:T(8,128)S(1)}) custom-call(s32[1]{0:T(128)} %bitcast.index_ref, f32[1024,1024]{1,0:T(8,128)S(1)} %copy-done.1, f32[1024,768]{1,0:T(8,128)S(1)} %shard_map.39.x_ref.tail_ref), custom_call_target="tpu_custom_call" | custom-call | flops 2013265920 | bytes 8650752 | tf_op jit(solution)/shard_map/pallas_call | solution.py:129
  34.3 4.4 %shard_map.40 = (f32[128,1152]{1,0:T(8,128)S(1)}, f32[128,1024]{1,0:T(8,128)S(1)}) custom-call(f32[128,1152]{1,0:T(8,128)S(1)} %copy-done.2, f32[128,1152]{1,0:T(8,128)S(1)} %collective-permute-done.got_ref), custom_call_target="tpu_custom_call" | custom-call | flops 281018368 | bytes 2293760 | tf_op jit(solution)/shard_map/pallas_call | solution.py:129
  39.4 7.7 %collective-permute-done.2 = f32[64,1024]{1,0:T(8,128)S(1)} collective-permute-done((f32[64,1024]{1,0:T(8,128)S(1)}, f32[64,1024]{1,0:T(8,128)S(1)}, u32[]{:S(2)}, u32[]{:S(2)}) %collective-permute-start.2) | collective-permute-done | bytes 262176 | tf_op jit(solution)/shard_map/ppermute | solution.py:20
  49.4 4.4 %shard_map.42 = (f32[128,1024]{1,0:T(8,128)S(1)}, f32[128,896]{1,0:T(8,128)S(1)}) custom-call(s32[1]{0:T(128)} %bitcast.index_ref, f32[64,1024]{1,0:T(8,128)S(1)} %add.30.own_ref, f32[64,1024]{1,0:T(8,128)S(1)} %collective-permute-done.3.got_ref), custom_call_target="tpu_custom_call" | custom-call | flops 268435456 | bytes 1507328 | tf_op jit(solution)/shard_map/pallas_call | solution.py:129
  63.7 3.4 %collective-permute-start.6 = (f32[64,896]{1,0:T(8,128)S(1)}, f32[64,896]{1,0:T(8,128)S(1)}, u32[]{:S(2)}, u32[]{:S(2)}) collective-permute-start(f32[64,896]{1,0:T(8,128)S(1)} %add.31.own_ref), channel_id=1, source_target_pairs={{0,1},{1,0},{2,3},{3,2},{4,5},{5,4},{6,7},{7,6},{8,9},{9,8},{10,11... | collective-permute-start | bytes 688136 | tf_op jit(solution)/shard_map/ppermute | solution.py:20
  67.2 4.8 %collective-permute-done.9 = f32[16,2560]{1,0:T(8,128)S(1)} collective-permute-done((f32[16,2560]{1,0:T(8,128)S(1)}, f32[16,2560]{1,0:T(8,128)S(1)}, u32[]{:S(2)}, u32[]{:S(2)}) %collective-permute-start.9) | collective-permute-done | bytes 163872 | tf_op jit(solution)/shard_map/ppermute | solution.py:20
  72.1 4.3 %shard_map.44 = (f32[128,896]{1,0:T(8,128)S(1)}, f32[128,768]{1,0:T(8,128)S(1)}) custom-call(s32[1]{0:T(128)} %bitcast.index_ref, f32[64,896]{1,0:T(8,128)S(1)} %add.31.own_ref, f32[64,896]{1,0:T(8,128)S(1)} %collective-permute-done.6.got_ref), custom_call_target="tpu_custom_call" | custom-call | flops 255852544 | bytes 1310720 | tf_op jit(solution)/shard_map/pallas_call | solution.py:129
  77.5 5.0 %collective-permute-done.11 = f32[16,2560]{1,0:T(8,128)S(1)} collective-permute-done((f32[16,2560]{1,0:T(8,128)S(1)}, f32[16,2560]{1,0:T(8,128)S(1)}, u32[]{:S(2)}, u32[]{:S(2)}) %collective-permute-start.11) | collective-permute-done | bytes 163872 | tf_op jit(solution)/shard_map/ppermute | solution.py:20
  92.8 4.3 %shard_map.49 = (f32[128,768]{1,0:T(8,128)S(1)}, f32[128,640]{1,0:T(8,128)S(1)}) custom-call(s32[1]{0:T(128)} %bitcast.index_ref, f32[4,16,768]{2,1,0:T(8,128)S(1)} %pad_maximum_fusion.1.own_ref, f32[4,16,768]{2,1,0:T(8,128)S(1)} %collective-permute-done.15.got_ref), custom_call_target="tpu_custom_call" | custom-call | flops 243269632 | bytes 1114112 | tf_op jit(solution)/shard_map/pallas_call | solution.py:129
  97.7 3.1 %collective-permute-start.16 = (f32[16,1792]{1,0:T(8,128)S(1)}, f32[16,1792]{1,0:T(8,128)S(1)}, u32[]{:S(2)}, u32[]{:S(2)}) collective-permute-start(f32[16,1792]{1,0:T(8,128)S(1)} %shard_map.51), channel_id=1, source_target_pairs={{0,16},{1,17},{2,18},{3,19},{4,20},{5,21},{6,22},{7,23},{8,24},{9,... | collective-permute-start | bytes 344072 | tf_op jit(solution)/shard_map/ppermute | solution.py:20
  100.8 5.6 %collective-permute-done.16 = f32[16,1792]{1,0:T(8,128)S(1)} collective-permute-done((f32[16,1792]{1,0:T(8,128)S(1)}, f32[16,1792]{1,0:T(8,128)S(1)}, u32[]{:S(2)}, u32[]{:S(2)}) %collective-permute-start.16) | collective-permute-done | bytes 114720 | tf_op jit(solution)/shard_map/ppermute | solution.py:20
  111.7 3.2 %collective-permute-start.20 = (f32[4,16,640]{2,1,0:T(8,128)S(1)}, f32[4,16,640]{2,1,0:T(8,128)S(1)}, u32[]{:S(2)}, u32[]{:S(2)}) collective-permute-start(f32[4,16,640]{2,1,0:T(8,128)S(1)} %pad_maximum_fusion.2.own_ref), channel_id=1, source_target_pairs={{0,1},{1,0},{2,3},{3,2},{4,5},{5,4},{6,7},{7,6},{8,9},{9,8},{10,11... | collective-permute-start | bytes 491528 | tf_op jit(solution)/shard_map/ppermute | solution.py:20
  115.9 4.2 %shard_map.52 = (f32[128,640]{1,0:T(8,128)S(1)}, f32[128,512]{1,0:T(8,128)S(1)}) custom-call(s32[1]{0:T(128)} %bitcast.index_ref, f32[4,16,640]{2,1,0:T(8,128)S(1)} %pad_maximum_fusion.2.own_ref, f32[4,16,640]{2,1,0:T(8,128)S(1)} %collective-permute-done.20.got_ref), custom_call_target="tpu_custom_call" | custom-call | flops 230686720 | bytes 917504 | tf_op jit(solution)/shard_map/pallas_call | solution.py:129
  120.6 5.7 %collective-permute-start.21 = (f32[16,1152]{1,0:T(8,128)S(1)}, f32[16,1152]{1,0:T(8,128)S(1)}, u32[]{:S(2)}, u32[]{:S(2)}) collective-permute-start(f32[16,1152]{1,0:T(8,128)S(1)} %shard_map.54), channel_id=1, source_target_pairs={{0,32},{1,33},{2,34},{3,35},{4,36},{5,37},{6,38},{7,39},{8,40},{9,... | collective-permute-start | bytes 221192 | tf_op jit(solution)/shard_map/ppermute | solution.py:20
  133.1 2.7 %collective-permute-done.23 = f32[16,1152]{1,0:T(8,128)S(1)} collective-permute-done((f32[16,1152]{1,0:T(8,128)S(1)}, f32[16,1152]{1,0:T(8,128)S(1)}, u32[]{:S(2)}, u32[]{:S(2)}) %collective-permute-start.23) | collective-permute-done | bytes 73760 | tf_op jit(solution)/shard_map/ppermute | solution.py:20
  139.3 4.2 %shard_map.55 = (f32[128,512]{1,0:T(8,128)S(1)}, f32[128,384]{1,0:T(8,128)S(1)}) custom-call(s32[1]{0:T(128)} %bitcast.index_ref, f32[4,16,512]{2,1,0:T(8,128)S(1)} %slice.14.own_ref, f32[4,16,512]{2,1,0:T(8,128)S(1)} %collective-permute-done.25.got_ref), custom_call_target="tpu_custom_call" | custom-call | flops 218103808 | bytes 720896 | tf_op jit(solution)/shard_map/pallas_call | solution.py:129
  150.6 4.2 %shard_map.58 = (f32[128,384]{1,0:T(8,128)S(1)}, f32[128,256]{1,0:T(8,128)S(1)}) custom-call(s32[1]{0:T(128)} %bitcast.index_ref, f32[64,384]{1,0:T(8,128)S(1)} %add.38.own_ref, f32[64,384]{1,0:T(8,128)S(1)} %collective-permute-done.27.got_ref), custom_call_target="tpu_custom_call" | custom-call | flops 205520896 | bytes 524288 | tf_op jit(solution)/shard_map/pallas_call | solution.py:129
  155.0 2.7 %collective-permute-start.29 = (f32[64,256]{1,0:T(8,128)S(1)}, f32[64,256]{1,0:T(8,128)S(1)}, u32[]{:S(2)}, u32[]{:S(2)}) collective-permute-start(f32[64,256]{1,0:T(8,128)S(1)} %shard_map.60), channel_id=1, source_target_pairs={{0,128},{1,129},{2,130},{3,131},{4,132},{5,133},{6,134},{7,135},{8... | collective-permute-start | bytes 196616 | tf_op jit(solution)/shard_map/ppermute | solution.py:20
  157.7 4.2 %shard_map.50.solved_ref = f32[1024,640]{1,0:T(8,128)S(1)} custom-call(f32[1024,128]{1,0:T(8,128)S(1)} %copy-done.5, f32[1024,256]{1,0:T(8,128)S(1)} %get-tuple-element.39.x12_ref, f32[1024,768]{1,0:T(8,128)S(1)} %shard_map.39.x_ref.tail_ref, f32[128,1024]{1,0:T(8,128)S(1)} %get-tuple-element.41.w_ref.w0, f32[128,896]{1,0:T(8,128)S(1)} %get-tuple-element.48.w_ref.w1, ...), custom_call_target="tpu_custom_call" | custom-call | flops 2013265920 | bytes 9043968 | tf_op jit(solution)/shard_map/pallas_call | solution.py:129
  166.5 4.2 %shard_map.61 = (f32[128,256]{1,0:T(8,128)}, f32[128,128]{1,0:T(8,128)S(1)}) custom-call(s32[1]{0:T(128)} %bitcast.index_ref, f32[64,256]{1,0:T(8,128)S(1)} %add.39.own_ref, f32[64,256]{1,0:T(8,128)S(1)} %collective-permute-done.30.got_ref), custom_call_target="tpu_custom_call" | custom-call | flops 192937984 | bytes 327680 | tf_op jit(solution)/shard_map/pallas_call | solution.py:129
  (90 shorter events, 58.8 us)
Async XLA Ops:
  10.9 27.9 %collective-permute-start.1 = (f32[192,1024]{1,0:T(8,128)S(1)}, f32[192,1024]{1,0:T(8,128)S(1)}, u32[]{:S(2)}, u32[]{:S(2)}) collective-permute-start(f32[192,1024]{1,0:T(8,128)S(1)} %get-tuple-element.42.own_ref), channel_id=1, source_target_pairs={{0,1},{1,0},{2,3},{3,2},{4,5},{5,4},{6,7},{7,6},{8,9},{9,8},{10,11... | collective-permute-start | bytes 2359304 | tf_op jit(solution)/shard_map/ppermute | solution.py:20
  22.0 12.3 %collective-permute-start = (f32[128,1152]{1,0:T(8,128)}, f32[128,1152]{1,0:T(8,128)S(1)}, u32[]{:S(2)}, u32[]{:S(2)}) collective-permute-start(f32[128,1152]{1,0:T(8,128)} %get-tuple-element.40.own_ref), channel_id=1, source_target_pairs={{0,1},{1,0},{2,3},{3,2},{4,5},{5,4},{6,7},{7,6},{8,9},{9,8},{10,11... | collective-permute-start | bytes 1769480 | tf_op jit(solution)/shard_map/ppermute | solution.py:20
  33.8 23.5 %collective-permute-start.7 = (f32[64,2560]{1,0:T(8,128)S(1)}, f32[64,2560]{1,0:T(8,128)S(1)}, u32[]{:S(2)}, u32[]{:S(2)}) collective-permute-start(f32[64,2560]{1,0:T(8,128)S(1)} %get-tuple-element.53), channel_id=1, source_target_pairs={{0,1},{1,0},{2,3},{3,2},{4,5},{5,4},{6,7},{7,6},{8,9},{9,8},{10,11... | collective-permute-start | bytes 1966088 | tf_op jit(solution)/shard_map/ppermute | solution.py:20
  39.3 7.8 %collective-permute-start.2 = (f32[64,1024]{1,0:T(8,128)S(1)}, f32[64,1024]{1,0:T(8,128)S(1)}, u32[]{:S(2)}, u32[]{:S(2)}) collective-permute-start(f32[64,1024]{1,0:T(8,128)S(1)} %get-tuple-element.45), channel_id=1, source_target_pairs={{0,2},{1,3},{2,0},{3,1},{4,6},{5,7},{6,4},{7,5},{8,10},{9,11},{10,... | collective-permute-start | bytes 786440 | tf_op jit(solution)/shard_map/ppermute | solution.py:20
  48.2 7.1 %collective-permute-start.4 = (f32[64,896]{1,0:T(8,128)S(1)}, f32[64,896]{1,0:T(8,128)S(1)}, u32[]{:S(2)}, u32[]{:S(2)}) collective-permute-start(f32[64,896]{1,0:T(8,128)S(1)} %get-tuple-element.49.own_ref), channel_id=1, source_target_pairs={{0,2},{1,3},{2,0},{3,1},{4,6},{5,7},{6,4},{7,5},{8,10},{9,11},{10,... | collective-permute-start | bytes 688136 | tf_op jit(solution)/shard_map/ppermute | solution.py:20
  55.7 8.0 %collective-permute-start.5 = (f32[64,896]{1,0:T(8,128)S(1)}, f32[64,896]{1,0:T(8,128)S(1)}, u32[]{:S(2)}, u32[]{:S(2)}) collective-permute-start(f32[64,896]{1,0:T(8,128)S(1)} %shard_map.43), channel_id=1, source_target_pairs={{0,4},{1,5},{2,6},{3,7},{4,0},{5,1},{6,2},{7,3},{8,12},{9,13},{10,... | collective-permute-start | bytes 688136 | tf_op jit(solution)/shard_map/ppermute | solution.py:20
  58.8 8.4 %collective-permute-start.8 = (f32[16,2560]{1,0:T(8,128)S(1)}, f32[16,2560]{1,0:T(8,128)S(1)}, u32[]{:S(2)}, u32[]{:S(2)}) collective-permute-start(f32[16,2560]{1,0:T(8,128)S(1)} %get-tuple-element.56), channel_id=1, source_target_pairs={{0,4},{1,5},{2,6},{3,7},{4,0},{5,1},{6,2},{7,3},{8,12},{9,13},{10,... | collective-permute-start | bytes 491528 | tf_op jit(solution)/shard_map/ppermute | solution.py:20
  60.5 11.5 %collective-permute-start.9 = (f32[16,2560]{1,0:T(8,128)S(1)}, f32[16,2560]{1,0:T(8,128)S(1)}, u32[]{:S(2)}, u32[]{:S(2)}) collective-permute-start(f32[16,2560]{1,0:T(8,128)S(1)} %get-tuple-element.57), channel_id=1, source_target_pairs={{0,6},{1,7},{2,4},{3,5},{4,2},{5,3},{6,0},{7,1},{8,14},{9,15},{10,... | collective-permute-start | bytes 491528 | tf_op jit(solution)/shard_map/ppermute | solution.py:20
  61.6 10.4 %collective-permute-start.10 = (f32[16,2560]{1,0:T(8,128)S(1)}, f32[16,2560]{1,0:T(8,128)S(1)}, u32[]{:S(2)}, u32[]{:S(2)}) collective-permute-start(f32[16,2560]{1,0:T(8,128)S(1)} %get-tuple-element.58), channel_id=1, source_target_pairs={{0,2},{1,3},{2,0},{3,1},{4,6},{5,7},{6,4},{7,5},{8,10},{9,11},{10,... | collective-permute-start | bytes 491528 | tf_op jit(solution)/shard_map/ppermute | solution.py:20
  63.7 8.4 %collective-permute-start.6 = (f32[64,896]{1,0:T(8,128)S(1)}, f32[64,896]{1,0:T(8,128)S(1)}, u32[]{:S(2)}, u32[]{:S(2)}) collective-permute-start(f32[64,896]{1,0:T(8,128)S(1)} %add.31.own_ref), channel_id=1, source_target_pairs={{0,1},{1,0},{2,3},{3,2},{4,5},{5,4},{6,7},{7,6},{8,9},{9,8},{10,11... | collective-permute-start | bytes 688136 | tf_op jit(solution)/shard_map/ppermute | solution.py:20
  77.1 5.3 %collective-permute-start.11 = (f32[16,2560]{1,0:T(8,128)S(1)}, f32[16,2560]{1,0:T(8,128)S(1)}, u32[]{:S(2)}, u32[]{:S(2)}) collective-permute-start(f32[16,2560]{1,0:T(8,128)S(1)} %shard_map.48), channel_id=1, source_target_pairs={{0,8},{1,9},{2,10},{3,11},{4,12},{5,13},{6,14},{7,15},{8,0},{9,1},... | collective-permute-start | bytes 491528 | tf_op jit(solution)/shard_map/ppermute | solution.py:20
  82.5 4.5 %collective-permute-start.13 = (f32[16,768]{1,0:T(8,128)S(1)}, f32[16,768]{1,0:T(8,128)S(1)}, u32[]{:S(2)}, u32[]{:S(2)}) collective-permute-start(f32[16,768]{1,0:T(8,128)S(1)} %get-tuple-element.72), channel_id=1, source_target_pairs={{0,4},{1,5},{2,6},{3,7},{4,0},{5,1},{6,2},{7,3},{8,12},{9,13},{10,... | collective-permute-start | bytes 147464 | tf_op jit(solution)/shard_map/ppermute | solution.py:20
  84.6 4.7 %collective-permute-start.14 = (f32[16,768]{1,0:T(8,128)S(1)}, f32[16,768]{1,0:T(8,128)S(1)}, u32[]{:S(2)}, u32[]{:S(2)}) collective-permute-start(f32[16,768]{1,0:T(8,128)S(1)} %get-tuple-element.72), channel_id=1, source_target_pairs={{0,6},{1,7},{2,4},{3,5},{4,2},{5,3},{6,0},{7,1},{8,14},{9,15},{10,... | collective-permute-start | bytes 147464 | tf_op jit(solution)/shard_map/ppermute | solution.py:20
  97.7 8.7 %collective-permute-start.16 = (f32[16,1792]{1,0:T(8,128)S(1)}, f32[16,1792]{1,0:T(8,128)S(1)}, u32[]{:S(2)}, u32[]{:S(2)}) collective-permute-start(f32[16,1792]{1,0:T(8,128)S(1)} %shard_map.51), channel_id=1, source_target_pairs={{0,16},{1,17},{2,18},{3,19},{4,20},{5,21},{6,22},{7,23},{8,24},{9,... | collective-permute-start | bytes 344072 | tf_op jit(solution)/shard_map/ppermute | solution.py:20
  106.4 4.4 %collective-permute-start.18 = (f32[16,640]{1,0:T(8,128)S(1)}, f32[16,640]{1,0:T(8,128)S(1)}, u32[]{:S(2)}, u32[]{:S(2)}) collective-permute-start(f32[16,640]{1,0:T(8,128)S(1)} %get-tuple-element.74), channel_id=1, source_target_pairs={{0,4},{1,5},{2,6},{3,7},{4,0},{5,1},{6,2},{7,3},{8,12},{9,13},{10,... | collective-permute-start | bytes 122888 | tf_op jit(solution)/shard_map/ppermute | solution.py:20
  111.7 4.3 %collective-permute-start.20 = (f32[4,16,640]{2,1,0:T(8,128)S(1)}, f32[4,16,640]{2,1,0:T(8,128)S(1)}, u32[]{:S(2)}, u32[]{:S(2)}) collective-permute-start(f32[4,16,640]{2,1,0:T(8,128)S(1)} %pad_maximum_fusion.2.own_ref), channel_id=1, source_target_pairs={{0,1},{1,0},{2,3},{3,2},{4,5},{5,4},{6,7},{7,6},{8,9},{9,8},{10,11... | collective-permute-start | bytes 491528 | tf_op jit(solution)/shard_map/ppermute | solution.py:20
  120.6 7.9 %collective-permute-start.21 = (f32[16,1152]{1,0:T(8,128)S(1)}, f32[16,1152]{1,0:T(8,128)S(1)}, u32[]{:S(2)}, u32[]{:S(2)}) collective-permute-start(f32[16,1152]{1,0:T(8,128)S(1)} %shard_map.54), channel_id=1, source_target_pairs={{0,32},{1,33},{2,34},{3,35},{4,36},{5,37},{6,38},{7,39},{8,40},{9,... | collective-permute-start | bytes 221192 | tf_op jit(solution)/shard_map/ppermute | solution.py:20
  128.6 4.5 %collective-permute-start.24 = (f32[16,1152]{1,0:T(8,128)S(1)}, f32[16,1152]{1,0:T(8,128)S(1)}, u32[]{:S(2)}, u32[]{:S(2)}) collective-permute-start(f32[16,1152]{1,0:T(8,128)S(1)} %add.37), channel_id=1, source_target_pairs={{0,6},{1,7},{2,4},{3,5},{4,2},{5,3},{6,0},{7,1},{8,14},{9,15},{10,... | collective-permute-start | bytes 221192 | tf_op jit(solution)/shard_map/ppermute | solution.py:20
  131.1 4.7 %collective-permute-start.23 = (f32[16,1152]{1,0:T(8,128)S(1)}, f32[16,1152]{1,0:T(8,128)S(1)}, u32[]{:S(2)}, u32[]{:S(2)}) collective-permute-start(f32[16,1152]{1,0:T(8,128)S(1)} %add.37), channel_id=1, source_target_pairs={{0,4},{1,5},{2,6},{3,7},{4,0},{5,1},{6,2},{7,3},{8,12},{9,13},{10,... | collective-permute-start | bytes 221192 | tf_op jit(solution)/shard_map/ppermute | solution.py:20
  131.1 4.7 %collective-permute-start.22 = (f32[16,1152]{1,0:T(8,128)S(1)}, f32[16,1152]{1,0:T(8,128)S(1)}, u32[]{:S(2)}, u32[]{:S(2)}) collective-permute-start(f32[16,1152]{1,0:T(8,128)S(1)} %add.37), channel_id=1, source_target_pairs={{0,2},{1,3},{2,0},{3,1},{4,6},{5,7},{6,4},{7,5},{8,10},{9,11},{10,... | collective-permute-start | bytes 221192 | tf_op jit(solution)/shard_map/ppermute | solution.py:20
  143.9 4.1 %collective-permute-start.26 = (f32[64,384]{1,0:T(8,128)S(1)}, f32[64,384]{1,0:T(8,128)S(1)}, u32[]{:S(2)}, u32[]{:S(2)}) collective-permute-start(f32[64,384]{1,0:T(8,128)S(1)} %get-tuple-element.66), channel_id=1, source_target_pairs={{0,64},{1,65},{2,66},{3,67},{4,68},{5,69},{6,70},{7,71},{8,72},{9,... | collective-permute-start | bytes 294920 | tf_op jit(solution)/shard_map/ppermute | solution.py:20
  149.3 5.5 %collective-permute-start.28 = (f32[64,256]{1,0:T(8,128)S(1)}, f32[64,256]{1,0:T(8,128)S(1)}, u32[]{:S(2)}, u32[]{:S(2)}) collective-permute-start(f32[64,256]{1,0:T(8,128)S(1)} %get-tuple-element.68.own_ref), channel_id=1, source_target_pairs={{0,64},{1,65},{2,66},{3,67},{4,68},{5,69},{6,70},{7,71},{8,72},{9,... | collective-permute-start | bytes 196616 | tf_op jit(solution)/shard_map/ppermute | solution.py:20
  155.0 7.0 %collective-permute-start.29 = (f32[64,256]{1,0:T(8,128)S(1)}, f32[64,256]{1,0:T(8,128)S(1)}, u32[]{:S(2)}, u32[]{:S(2)}) collective-permute-start(f32[64,256]{1,0:T(8,128)S(1)} %shard_map.60), channel_id=1, source_target_pairs={{0,128},{1,129},{2,130},{3,131},{4,132},{5,133},{6,134},{7,135},{8... | collective-permute-start | bytes 196616 | tf_op jit(solution)/shard_map/ppermute | solution.py:20
  162.0 4.5 %collective-permute-start.30 = (f32[64,256]{1,0:T(8,128)S(1)}, f32[64,256]{1,0:T(8,128)S(1)}, u32[]{:S(2)}, u32[]{:S(2)}) collective-permute-start(f32[64,256]{1,0:T(8,128)S(1)} %add.39.own_ref), channel_id=1, source_target_pairs={{0,1},{1,0},{2,3},{3,2},{4,5},{5,4},{6,7},{7,6},{8,9},{9,8},{10,11... | collective-permute-start | bytes 196616 | tf_op jit(solution)/shard_map/ppermute | solution.py:20
  (13 other events, 103.7 us)

commit v3 on v1

--- a/solution.py
+++ b/solution.py
@@ -218,7 +218,7 @@
             pltpu.SemaphoreType.DMA((3,)),
         ],
         cost_estimate=pl.CostEstimate(flops=6 * leaf * R * 54 * R, bytes_accessed=8 * leaf * leaf, transcendentals=0),
-        compiler_params=pltpu.CompilerParams(vmem_limit_bytes=60 << 20),
+        compiler_params=pltpu.CompilerParams(vmem_limit_bytes=56 << 20),
     )(index, leaf_inverse, bases, white_noise)
 
 
@@ -288,6 +288,10 @@
     return call(kernel, outs, (own, got), index=index, flops=flops)
 
 
+def stage_kernel(rows_ref, staged_ref):
+    staged_ref[...] = rows_ref[...]
+
+
 def row1_kernel(index_ref, own_ref, got_ref, keep_ref, got2_ref, panel_ref, w_ref, row_ref, half_ref, half2_ref):
     core = index_ref[0] & 1
     w = split(w_ref[...])
@@ -375,6 +379,11 @@
     core = index_ref[0] & 1
     for _, _, _, change in downdate(core, 6, panel_ref, w_ref, row_blocks(7)[0]):
         row_ref[...] = own_ref[...] + got_ref[...] - change
+
+
+def last_kernel(solved_ref, w_ref, solution_ref):
+    first = dot_split(split(solved_ref[:, :R]), split(w_ref[...]))
+    solution_ref[...] = solved_ref[:, R:] - first
 
 
 def solve_step_kernel(solved_ref, w_ref, next_ref):
@@ -422,6 +431,7 @@
     leaf = leaf_inverse.shape[0]
     x_head, rows01, keep2, send2 = head(index, leaf_inverse, bases, white_noise)
     got01 = swap(rows01, CORE_MASK)
+    (rows01,) = call(stage_kernel, (out(R, 17 * R),), (rows01,))
     got2 = swap(send2, CORE_MASK)
     weights = []
     panel, w = invert(0, rows01, got01, index)
@@ -524,7 +534,8 @@
     got = swap(half, 128)
     half = half + got
     _, w = invert(7, half, swap(half, CORE_MASK), index)
-    return solve_step(solved, w)
+    (answer,) = call(last_kernel, (out(leaf, R),), (solved, w), flops=6 * leaf * R * R)
+    return answer
 
 
 def solution(mesh):

time: 165 us -> 162 us (0.982)
  local copies, waits for them, and re-layouts: 4.42 us -> 2.24 us
    unnamed x14, local copies, waits for them, and re-layouts: 4.4 us -> 2.21 us
    pallas_call x24 -> x25, Pallas kernels: 57.9 us -> 57.6 us  [call(): pl.pallas_call(kernel, out_shape=outs, in_specs=(smem() if head else [])...]
where the time goes in v3:
time: 162 us
  Pallas kernels  69.1 us (43%)
  starting transfers between devices  49.7 us (31%)
  waiting for transfers between devices  40.4 us (25%)
  local copies, waits for them, and re-layouts  2.24 us (1%)
    pallas_call x25, Pallas kernels, call(): pl.pallas_call(kernel, out_shape=outs, in_specs=(smem() if head else [])...  57.6 us
    ppermute x31, starting transfers between devices, swap(): lax.ppermute(value, 'leaf', [(i, i ^ mask) for i in range(lax.axis_size('...  49.7 us
    ppermute x31, waiting for transfers between devices, swap(): lax.ppermute(value, 'leaf', [(i, i ^ mask) for i in range(lax.axis_size('...  40.4 us
    pallas_call x1, Pallas kernels, head(): pl.pallas_call(head_kernel, name='head', out_shape=(out(leaf, HEAD), out(...  11.5 us
  transfers between devices with their start and end apart: 31, of which 19 were waited for; matrix products, arithmetic and copies ran while one was open for 0% of the time, Pallas kernels for 20%

profile of v3, /device:TPU:1, one launch (start us, length us, event | category | flops | bytes accessed | tf_op | source)
XLA Modules:
  0.0 162.0 jit_solution(4235116706725077820)
XLA Ops:
  0.0 11.5 %head.1 = (f32[1024,384]{1,0:T(8,128)}, f32[128,2176]{1,0:T(8,128)}, f32[64,896]{1,0:T(8,128)}, f32[64,896]{1,0:T(8,128)}) custom-call(s32[1]{0:T(128)} %bitcast.index_ref, f32[1024,1024]{1,0:T(8,128)} %a_ref.1, f32[1024,1024]{1,0:T(8,128)} %u_ref.3, f32[1024,128]{1,0:T(8,128)} %w_ref.1), custom_call_target="tpu_custom_call" | custom-call | flops 5435817984 | bytes 8388608 | tf_op jit(solution)/shard_map/head/pallas_call | solution.py:204
  11.6 3.3 %collective-permute-start = (f32[128,2176]{1,0:T(8,128)}, f32[128,2176]{1,0:T(8,128)S(1)}, u32[]{:S(2)}, u32[]{:S(2)}) collective-permute-start(f32[128,2176]{1,0:T(8,128)} %get-tuple-element.38.rows_ref), channel_id=1, source_target_pairs={{0,1},{1,0},{2,3},{3,2},{4,5},{5,4},{6,7},{7,6},{8,9},{9,8},{10,11... | collective-permute-start | bytes 3342344 | tf_op jit(solution)/shard_map/ppermute | solution.py:20
  17.1 6.1 %shard_map.37.x_ref.tail_ref = f32[1024,768]{1,0:T(8,128)S(1)} custom-call(f32[1024,1024]{1,0:T(8,128)S(1)} %copy-done.3, f32[1024,1024]{1,0:T(8,128)S(1)} %copy-done.4, f32[1024,128]{1,0:T(8,128)S(1)} %copy-done.6), custom_call_target="tpu_custom_call" | custom-call | flops 4831838208 | bytes 12058624 | tf_op jit(solution)/shard_map/pallas_call | solution.py:129
  23.3 2.5 %shard_map.44 = (f32[64,2560]{1,0:T(8,128)S(1)}, f32[64,2560]{1,0:T(8,128)S(1)}) custom-call(s32[1]{0:T(128)} %bitcast.index_ref, f32[1024,1024]{1,0:T(8,128)S(1)} %copy-done.5, f32[1024,768]{1,0:T(8,128)S(1)} %shard_map.37.x_ref.tail_ref), custom_call_target="tpu_custom_call" | custom-call | flops 2013265920 | bytes 8650752 | tf_op jit(solution)/shard_map/pallas_call | solution.py:129
  26.4 4.4 %shard_map.39 = (f32[128,1152]{1,0:T(8,128)S(1)}, f32[128,1024]{1,0:T(8,128)S(1)}) custom-call(f32[128,2176]{1,0:T(8,128)S(1)} %shard_map.38.own_ref, f32[128,2176]{1,0:T(8,128)S(1)} %collective-permute-done.got_ref), custom_call_target="tpu_custom_call" | custom-call | flops 281018368 | bytes 3342336 | tf_op jit(solution)/shard_map/pallas_call | solution.py:129
  31.5 7.7 %collective-permute-done.2 = f32[64,1024]{1,0:T(8,128)S(1)} collective-permute-done((f32[64,1024]{1,0:T(8,128)S(1)}, f32[64,1024]{1,0:T(8,128)S(1)}, u32[]{:S(2)}, u32[]{:S(2)}) %collective-permute-start.2) | collective-permute-done | bytes 262176 | tf_op jit(solution)/shard_map/ppermute | solution.py:20
  41.5 4.4 %shard_map.41 = (f32[128,1024]{1,0:T(8,128)S(1)}, f32[128,896]{1,0:T(8,128)S(1)}) custom-call(s32[1]{0:T(128)} %bitcast.index_ref, f32[64,1024]{1,0:T(8,128)S(1)} %add.30.own_ref, f32[64,1024]{1,0:T(8,128)S(1)} %collective-permute-done.3.got_ref), custom_call_target="tpu_custom_call" | custom-call | flops 268435456 | bytes 1507328 | tf_op jit(solution)/shard_map/pallas_call | solution.py:129
  55.3 3.7 %collective-permute-start.6 = (f32[64,896]{1,0:T(8,128)S(1)}, f32[64,896]{1,0:T(8,128)S(1)}, u32[]{:S(2)}, u32[]{:S(2)}) collective-permute-start(f32[64,896]{1,0:T(8,128)S(1)} %add.31.own_ref), channel_id=1, source_target_pairs={{0,1},{1,0},{2,3},{3,2},{4,5},{5,4},{6,7},{7,6},{8,9},{9,8},{10,11... | collective-permute-start | bytes 688136 | tf_op jit(solution)/shard_map/ppermute | solution.py:20
  62.3 4.3 %shard_map.43 = (f32[128,896]{1,0:T(8,128)S(1)}, f32[128,768]{1,0:T(8,128)S(1)}) custom-call(s32[1]{0:T(128)} %bitcast.index_ref, f32[64,896]{1,0:T(8,128)S(1)} %add.31.own_ref, f32[64,896]{1,0:T(8,128)S(1)} %collective-permute-done.6.got_ref), custom_call_target="tpu_custom_call" | custom-call | flops 255852544 | bytes 1310720 | tf_op jit(solution)/shard_map/pallas_call | solution.py:129
  67.5 4.1 %collective-permute-done.11 = f32[16,2560]{1,0:T(8,128)S(1)} collective-permute-done((f32[16,2560]{1,0:T(8,128)S(1)}, f32[16,2560]{1,0:T(8,128)S(1)}, u32[]{:S(2)}, u32[]{:S(2)}) %collective-permute-start.11) | collective-permute-done | bytes 163872 | tf_op jit(solution)/shard_map/ppermute | solution.py:20
  77.1 4.7 %collective-permute-start.15 = (f32[4,16,768]{2,1,0:T(8,128)S(1)}, f32[4,16,768]{2,1,0:T(8,128)S(1)}, u32[]{:S(2)}, u32[]{:S(2)}) collective-permute-start(f32[4,16,768]{2,1,0:T(8,128)S(1)} %pad_maximum_fusion.1.own_ref), channel_id=1, source_target_pairs={{0,1},{1,0},{2,3},{3,2},{4,5},{5,4},{6,7},{7,6},{8,9},{9,8},{10,11... | collective-permute-start | bytes 589832 | tf_op jit(solution)/shard_map/ppermute | solution.py:20
  83.0 4.3 %shard_map.48 = (f32[128,768]{1,0:T(8,128)S(1)}, f32[128,640]{1,0:T(8,128)S(1)}) custom-call(s32[1]{0:T(128)} %bitcast.index_ref, f32[4,16,768]{2,1,0:T(8,128)S(1)} %pad_maximum_fusion.1.own_ref, f32[4,16,768]{2,1,0:T(8,128)S(1)} %collective-permute-done.15.got_ref), custom_call_target="tpu_custom_call" | custom-call | flops 243269632 | bytes 1114112 | tf_op jit(solution)/shard_map/pallas_call | solution.py:129
  87.8 2.8 %collective-permute-start.16 = (f32[16,1792]{1,0:T(8,128)S(1)}, f32[16,1792]{1,0:T(8,128)S(1)}, u32[]{:S(2)}, u32[]{:S(2)}) collective-permute-start(f32[16,1792]{1,0:T(8,128)S(1)} %shard_map.50), channel_id=1, source_target_pairs={{0,16},{1,17},{2,18},{3,19},{4,20},{5,21},{6,22},{7,23},{8,24},{9,... | collective-permute-start | bytes 344072 | tf_op jit(solution)/shard_map/ppermute | solution.py:20
  90.6 5.6 %collective-permute-done.16 = f32[16,1792]{1,0:T(8,128)S(1)} collective-permute-done((f32[16,1792]{1,0:T(8,128)S(1)}, f32[16,1792]{1,0:T(8,128)S(1)}, u32[]{:S(2)}, u32[]{:S(2)}) %collective-permute-start.16) | collective-permute-done | bytes 114720 | tf_op jit(solution)/shard_map/ppermute | solution.py:20
  101.8 2.7 %collective-permute-start.20 = (f32[4,16,640]{2,1,0:T(8,128)S(1)}, f32[4,16,640]{2,1,0:T(8,128)S(1)}, u32[]{:S(2)}, u32[]{:S(2)}) collective-permute-start(f32[4,16,640]{2,1,0:T(8,128)S(1)} %pad_maximum_fusion.2.own_ref), channel_id=1, source_target_pairs={{0,1},{1,0},{2,3},{3,2},{4,5},{5,4},{6,7},{7,6},{8,9},{9,8},{10,11... | collective-permute-start | bytes 491528 | tf_op jit(solution)/shard_map/ppermute | solution.py:20
  105.5 4.2 %shard_map.51 = (f32[128,640]{1,0:T(8,128)S(1)}, f32[128,512]{1,0:T(8,128)S(1)}) custom-call(s32[1]{0:T(128)} %bitcast.index_ref, f32[4,16,640]{2,1,0:T(8,128)S(1)} %pad_maximum_fusion.2.own_ref, f32[4,16,640]{2,1,0:T(8,128)S(1)} %collective-permute-done.20.got_ref), custom_call_target="tpu_custom_call" | custom-call | flops 230686720 | bytes 917504 | tf_op jit(solution)/shard_map/pallas_call | solution.py:129
  110.2 6.2 %collective-permute-start.21 = (f32[16,1152]{1,0:T(8,128)S(1)}, f32[16,1152]{1,0:T(8,128)S(1)}, u32[]{:S(2)}, u32[]{:S(2)}) collective-permute-start(f32[16,1152]{1,0:T(8,128)S(1)} %shard_map.53), channel_id=1, source_target_pairs={{0,32},{1,33},{2,34},{3,35},{4,36},{5,37},{6,38},{7,39},{8,40},{9,... | collective-permute-start | bytes 221192 | tf_op jit(solution)/shard_map/ppermute | solution.py:20
  125.2 2.4 %collective-permute-start.25 = (f32[4,16,512]{2,1,0:T(8,128)S(1)}, f32[4,16,512]{2,1,0:T(8,128)S(1)}, u32[]{:S(2)}, u32[]{:S(2)}) collective-permute-start(f32[4,16,512]{2,1,0:T(8,128)S(1)} %slice.14.own_ref), channel_id=1, source_target_pairs={{0,1},{1,0},{2,3},{3,2},{4,5},{5,4},{6,7},{7,6},{8,9},{9,8},{10,11... | collective-permute-start | bytes 393224 | tf_op jit(solution)/shard_map/ppermute | solution.py:20
  128.6 4.2 %shard_map.54 = (f32[128,512]{1,0:T(8,128)S(1)}, f32[128,384]{1,0:T(8,128)S(1)}) custom-call(s32[1]{0:T(128)} %bitcast.index_ref, f32[4,16,512]{2,1,0:T(8,128)S(1)} %slice.14.own_ref, f32[4,16,512]{2,1,0:T(8,128)S(1)} %collective-permute-done.25.got_ref), custom_call_target="tpu_custom_call" | custom-call | flops 218103808 | bytes 720896 | tf_op jit(solution)/shard_map/pallas_call | solution.py:129
  134.5 2.7 %collective-permute-done.26 = f32[64,384]{1,0:T(8,128)S(1)} collective-permute-done((f32[64,384]{1,0:T(8,128)S(1)}, f32[64,384]{1,0:T(8,128)S(1)}, u32[]{:S(2)}, u32[]{:S(2)}) %collective-permute-start.26) | collective-permute-done | bytes 98336 | tf_op jit(solution)/shard_map/ppermute | solution.py:20
  139.8 4.2 %shard_map.57 = (f32[128,384]{1,0:T(8,128)S(1)}, f32[128,256]{1,0:T(8,128)S(1)}) custom-call(s32[1]{0:T(128)} %bitcast.index_ref, f32[64,384]{1,0:T(8,128)S(1)} %add.38.own_ref, f32[64,384]{1,0:T(8,128)S(1)} %collective-permute-done.27.got_ref), custom_call_target="tpu_custom_call" | custom-call | flops 205520896 | bytes 524288 | tf_op jit(solution)/shard_map/pallas_call | solution.py:129
  144.3 2.7 %collective-permute-start.29 = (f32[64,256]{1,0:T(8,128)S(1)}, f32[64,256]{1,0:T(8,128)S(1)}, u32[]{:S(2)}, u32[]{:S(2)}) collective-permute-start(f32[64,256]{1,0:T(8,128)S(1)} %shard_map.59), channel_id=1, source_target_pairs={{0,128},{1,129},{2,130},{3,131},{4,132},{5,133},{6,134},{7,135},{8... | collective-permute-start | bytes 196616 | tf_op jit(solution)/shard_map/ppermute | solution.py:20
  147.0 5.0 %shard_map.49.solved_ref = f32[1024,640]{1,0:T(8,128)S(1)} custom-call(f32[1024,384]{1,0:T(8,128)S(1)} %copy-done, f32[1024,768]{1,0:T(8,128)S(1)} %shard_map.37.x_ref.tail_ref, f32[128,1024]{1,0:T(8,128)S(1)} %get-tuple-element.39.w_ref.w0, f32[128,896]{1,0:T(8,128)S(1)} %get-tuple-element.46.w_ref.w1, f32[128,768]{1,0:T(8,128)S(1)} %get-tuple-element.49.w_ref.w2, ...), custom_call_target="tpu_custom_call" | custom-call | flops 2013265920 | bytes 9043968 | tf_op jit(solution)/shard_map/pallas_call | solution.py:129
  156.6 4.2 %shard_map.60 = (f32[128,256]{1,0:T(8,128)}, f32[128,128]{1,0:T(8,128)S(1)}) custom-call(s32[1]{0:T(128)} %bitcast.index_ref, f32[64,256]{1,0:T(8,128)S(1)} %add.39.own_ref, f32[64,256]{1,0:T(8,128)S(1)} %collective-permute-done.30.got_ref), custom_call_target="tpu_custom_call" | custom-call | flops 192937984 | bytes 327680 | tf_op jit(solution)/shard_map/pallas_call | solution.py:129
  (92 shorter events, 53.5 us)
Async XLA Ops:
  11.6 14.8 %collective-permute-start = (f32[128,2176]{1,0:T(8,128)}, f32[128,2176]{1,0:T(8,128)S(1)}, u32[]{:S(2)}, u32[]{:S(2)}) collective-permute-start(f32[128,2176]{1,0:T(8,128)} %get-tuple-element.38.rows_ref), channel_id=1, source_target_pairs={{0,1},{1,0},{2,3},{3,2},{4,5},{5,4},{6,7},{7,6},{8,9},{9,8},{10,11... | collective-permute-start | bytes 3342344 | tf_op jit(solution)/shard_map/ppermute | solution.py:20
  14.8 16.0 %collective-permute-start.1 = (f32[64,896]{1,0:T(8,128)}, f32[64,896]{1,0:T(8,128)S(1)}, u32[]{:S(2)}, u32[]{:S(2)}) collective-permute-start(f32[64,896]{1,0:T(8,128)} %get-tuple-element.41), channel_id=1, source_target_pairs={{0,1},{1,0},{2,3},{3,2},{4,5},{5,4},{6,7},{7,6},{8,9},{9,8},{10,11... | collective-permute-start | bytes 688136 | tf_op jit(solution)/shard_map/ppermute | solution.py:20
  25.8 22.9 %collective-permute-start.7 = (f32[64,2560]{1,0:T(8,128)S(1)}, f32[64,2560]{1,0:T(8,128)S(1)}, u32[]{:S(2)}, u32[]{:S(2)}) collective-permute-start(f32[64,2560]{1,0:T(8,128)S(1)} %get-tuple-element.51), channel_id=1, source_target_pairs={{0,1},{1,0},{2,3},{3,2},{4,5},{5,4},{6,7},{7,6},{8,9},{9,8},{10,11... | collective-permute-start | bytes 1966088 | tf_op jit(solution)/shard_map/ppermute | solution.py:20
  31.4 7.8 %collective-permute-start.2 = (f32[64,1024]{1,0:T(8,128)S(1)}, f32[64,1024]{1,0:T(8,128)S(1)}, u32[]{:S(2)}, u32[]{:S(2)}) collective-permute-start(f32[64,1024]{1,0:T(8,128)S(1)} %get-tuple-element.43), channel_id=1, source_target_pairs={{0,2},{1,3},{2,0},{3,1},{4,6},{5,7},{6,4},{7,5},{8,10},{9,11},{10,... | collective-permute-start | bytes 786440 | tf_op jit(solution)/shard_map/ppermute | solution.py:20
  40.4 6.9 %collective-permute-start.4 = (f32[64,896]{1,0:T(8,128)S(1)}, f32[64,896]{1,0:T(8,128)S(1)}, u32[]{:S(2)}, u32[]{:S(2)}) collective-permute-start(f32[64,896]{1,0:T(8,128)S(1)} %get-tuple-element.47.own_ref), channel_id=1, source_target_pairs={{0,2},{1,3},{2,0},{3,1},{4,6},{5,7},{6,4},{7,5},{8,10},{9,11},{10,... | collective-permute-start | bytes 688136 | tf_op jit(solution)/shard_map/ppermute | solution.py:20
  47.6 7.6 %collective-permute-start.5 = (f32[64,896]{1,0:T(8,128)S(1)}, f32[64,896]{1,0:T(8,128)S(1)}, u32[]{:S(2)}, u32[]{:S(2)}) collective-permute-start(f32[64,896]{1,0:T(8,128)S(1)} %shard_map.42), channel_id=1, source_target_pairs={{0,4},{1,5},{2,6},{3,7},{4,0},{5,1},{6,2},{7,3},{8,12},{9,13},{10,... | collective-permute-start | bytes 688136 | tf_op jit(solution)/shard_map/ppermute | solution.py:20
  50.3 8.7 %collective-permute-start.10 = (f32[16,2560]{1,0:T(8,128)S(1)}, f32[16,2560]{1,0:T(8,128)S(1)}, u32[]{:S(2)}, u32[]{:S(2)}) collective-permute-start(f32[16,2560]{1,0:T(8,128)S(1)} %get-tuple-element.56), channel_id=1, source_target_pairs={{0,2},{1,3},{2,0},{3,1},{4,6},{5,7},{6,4},{7,5},{8,10},{9,11},{10,... | collective-permute-start | bytes 491528 | tf_op jit(solution)/shard_map/ppermute | solution.py:20
  50.7 9.8 %collective-permute-start.9 = (f32[16,2560]{1,0:T(8,128)S(1)}, f32[16,2560]{1,0:T(8,128)S(1)}, u32[]{:S(2)}, u32[]{:S(2)}) collective-permute-start(f32[16,2560]{1,0:T(8,128)S(1)} %get-tuple-element.55), channel_id=1, source_target_pairs={{0,6},{1,7},{2,4},{3,5},{4,2},{5,3},{6,0},{7,1},{8,14},{9,15},{10,... | collective-permute-start | bytes 491528 | tf_op jit(solution)/shard_map/ppermute | solution.py:20
  52.6 9.7 %collective-permute-start.8 = (f32[16,2560]{1,0:T(8,128)S(1)}, f32[16,2560]{1,0:T(8,128)S(1)}, u32[]{:S(2)}, u32[]{:S(2)}) collective-permute-start(f32[16,2560]{1,0:T(8,128)S(1)} %get-tuple-element.54), channel_id=1, source_target_pairs={{0,4},{1,5},{2,6},{3,7},{4,0},{5,1},{6,2},{7,3},{8,12},{9,13},{10,... | collective-permute-start | bytes 491528 | tf_op jit(solution)/shard_map/ppermute | solution.py:20
  55.3 7.0 %collective-permute-start.6 = (f32[64,896]{1,0:T(8,128)S(1)}, f32[64,896]{1,0:T(8,128)S(1)}, u32[]{:S(2)}, u32[]{:S(2)}) collective-permute-start(f32[64,896]{1,0:T(8,128)S(1)} %add.31.own_ref), channel_id=1, source_target_pairs={{0,1},{1,0},{2,3},{3,2},{4,5},{5,4},{6,7},{7,6},{8,9},{9,8},{10,11... | collective-permute-start | bytes 688136 | tf_op jit(solution)/shard_map/ppermute | solution.py:20
  67.4 4.3 %collective-permute-start.11 = (f32[16,2560]{1,0:T(8,128)S(1)}, f32[16,2560]{1,0:T(8,128)S(1)}, u32[]{:S(2)}, u32[]{:S(2)}) collective-permute-start(f32[16,2560]{1,0:T(8,128)S(1)} %shard_map.47), channel_id=1, source_target_pairs={{0,8},{1,9},{2,10},{3,11},{4,12},{5,13},{6,14},{7,15},{8,0},{9,1},... | collective-permute-start | bytes 491528 | tf_op jit(solution)/shard_map/ppermute | solution.py:20
  71.6 4.2 %collective-permute-start.14 = (f32[16,768]{1,0:T(8,128)S(1)}, f32[16,768]{1,0:T(8,128)S(1)}, u32[]{:S(2)}, u32[]{:S(2)}) collective-permute-start(f32[16,768]{1,0:T(8,128)S(1)} %get-tuple-element.70), channel_id=1, source_target_pairs={{0,6},{1,7},{2,4},{3,5},{4,2},{5,3},{6,0},{7,1},{8,14},{9,15},{10,... | collective-permute-start | bytes 147464 | tf_op jit(solution)/shard_map/ppermute | solution.py:20
  72.7 4.4 %collective-permute-start.13 = (f32[16,768]{1,0:T(8,128)S(1)}, f32[16,768]{1,0:T(8,128)S(1)}, u32[]{:S(2)}, u32[]{:S(2)}) collective-permute-start(f32[16,768]{1,0:T(8,128)S(1)} %get-tuple-element.70), channel_id=1, source_target_pairs={{0,4},{1,5},{2,6},{3,7},{4,0},{5,1},{6,2},{7,3},{8,12},{9,13},{10,... | collective-permute-start | bytes 147464 | tf_op jit(solution)/shard_map/ppermute | solution.py:20
  77.1 5.8 %collective-permute-start.15 = (f32[4,16,768]{2,1,0:T(8,128)S(1)}, f32[4,16,768]{2,1,0:T(8,128)S(1)}, u32[]{:S(2)}, u32[]{:S(2)}) collective-permute-start(f32[4,16,768]{2,1,0:T(8,128)S(1)} %pad_maximum_fusion.1.own_ref), channel_id=1, source_target_pairs={{0,1},{1,0},{2,3},{3,2},{4,5},{5,4},{6,7},{7,6},{8,9},{9,8},{10,11... | collective-permute-start | bytes 589832 | tf_op jit(solution)/shard_map/ppermute | solution.py:20
  87.8 8.4 %collective-permute-start.16 = (f32[16,1792]{1,0:T(8,128)S(1)}, f32[16,1792]{1,0:T(8,128)S(1)}, u32[]{:S(2)}, u32[]{:S(2)}) collective-permute-start(f32[16,1792]{1,0:T(8,128)S(1)} %shard_map.50), channel_id=1, source_target_pairs={{0,16},{1,17},{2,18},{3,19},{4,20},{5,21},{6,22},{7,23},{8,24},{9,... | collective-permute-start | bytes 344072 | tf_op jit(solution)/shard_map/ppermute | solution.py:20
  96.3 4.2 %collective-permute-start.19 = (f32[16,640]{1,0:T(8,128)S(1)}, f32[16,640]{1,0:T(8,128)S(1)}, u32[]{:S(2)}, u32[]{:S(2)}) collective-permute-start(f32[16,640]{1,0:T(8,128)S(1)} %get-tuple-element.72), channel_id=1, source_target_pairs={{0,6},{1,7},{2,4},{3,5},{4,2},{5,3},{6,0},{7,1},{8,14},{9,15},{10,... | collective-permute-start | bytes 122888 | tf_op jit(solution)/shard_map/ppermute | solution.py:20
  97.4 4.4 %collective-permute-start.18 = (f32[16,640]{1,0:T(8,128)S(1)}, f32[16,640]{1,0:T(8,128)S(1)}, u32[]{:S(2)}, u32[]{:S(2)}) collective-permute-start(f32[16,640]{1,0:T(8,128)S(1)} %get-tuple-element.72), channel_id=1, source_target_pairs={{0,4},{1,5},{2,6},{3,7},{4,0},{5,1},{6,2},{7,3},{8,12},{9,13},{10,... | collective-permute-start | bytes 122888 | tf_op jit(solution)/shard_map/ppermute | solution.py:20
  110.2 8.5 %collective-permute-start.21 = (f32[16,1152]{1,0:T(8,128)S(1)}, f32[16,1152]{1,0:T(8,128)S(1)}, u32[]{:S(2)}, u32[]{:S(2)}) collective-permute-start(f32[16,1152]{1,0:T(8,128)S(1)} %shard_map.53), channel_id=1, source_target_pairs={{0,32},{1,33},{2,34},{3,35},{4,36},{5,37},{6,38},{7,39},{8,40},{9,... | collective-permute-start | bytes 221192 | tf_op jit(solution)/shard_map/ppermute | solution.py:20
  118.7 4.5 %collective-permute-start.24 = (f32[16,1152]{1,0:T(8,128)S(1)}, f32[16,1152]{1,0:T(8,128)S(1)}, u32[]{:S(2)}, u32[]{:S(2)}) collective-permute-start(f32[16,1152]{1,0:T(8,128)S(1)} %add.37), channel_id=1, source_target_pairs={{0,6},{1,7},{2,4},{3,5},{4,2},{5,3},{6,0},{7,1},{8,14},{9,15},{10,... | collective-permute-start | bytes 221192 | tf_op jit(solution)/shard_map/ppermute | solution.py:20
  120.4 4.8 %collective-permute-start.23 = (f32[16,1152]{1,0:T(8,128)S(1)}, f32[16,1152]{1,0:T(8,128)S(1)}, u32[]{:S(2)}, u32[]{:S(2)}) collective-permute-start(f32[16,1152]{1,0:T(8,128)S(1)} %add.37), channel_id=1, source_target_pairs={{0,4},{1,5},{2,6},{3,7},{4,0},{5,1},{6,2},{7,3},{8,12},{9,13},{10,... | collective-permute-start | bytes 221192 | tf_op jit(solution)/shard_map/ppermute | solution.py:20
  133.1 4.1 %collective-permute-start.26 = (f32[64,384]{1,0:T(8,128)S(1)}, f32[64,384]{1,0:T(8,128)S(1)}, u32[]{:S(2)}, u32[]{:S(2)}) collective-permute-start(f32[64,384]{1,0:T(8,128)S(1)} %get-tuple-element.64), channel_id=1, source_target_pairs={{0,64},{1,65},{2,66},{3,67},{4,68},{5,69},{6,70},{7,71},{8,72},{9,... | collective-permute-start | bytes 294920 | tf_op jit(solution)/shard_map/ppermute | solution.py:20
  138.5 5.5 %collective-permute-start.28 = (f32[64,256]{1,0:T(8,128)S(1)}, f32[64,256]{1,0:T(8,128)S(1)}, u32[]{:S(2)}, u32[]{:S(2)}) collective-permute-start(f32[64,256]{1,0:T(8,128)S(1)} %get-tuple-element.66.own_ref), channel_id=1, source_target_pairs={{0,64},{1,65},{2,66},{3,67},{4,68},{5,69},{6,70},{7,71},{8,72},{9,... | collective-permute-start | bytes 196616 | tf_op jit(solution)/shard_map/ppermute | solution.py:20
  144.3 7.8 %collective-permute-start.29 = (f32[64,256]{1,0:T(8,128)S(1)}, f32[64,256]{1,0:T(8,128)S(1)}, u32[]{:S(2)}, u32[]{:S(2)}) collective-permute-start(f32[64,256]{1,0:T(8,128)S(1)} %shard_map.59), channel_id=1, source_target_pairs={{0,128},{1,129},{2,130},{3,131},{4,132},{5,133},{6,134},{7,135},{8... | collective-permute-start | bytes 196616 | tf_op jit(solution)/shard_map/ppermute | solution.py:20
  152.1 4.5 %collective-permute-start.30 = (f32[64,256]{1,0:T(8,128)S(1)}, f32[64,256]{1,0:T(8,128)S(1)}, u32[]{:S(2)}, u32[]{:S(2)}) collective-permute-start(f32[64,256]{1,0:T(8,128)S(1)} %add.39.own_ref), channel_id=1, source_target_pairs={{0,1},{1,0},{2,3},{3,2},{4,5},{5,4},{6,7},{7,6},{8,9},{9,8},{10,11... | collective-permute-start | bytes 196616 | tf_op jit(solution)/shard_map/ppermute | solution.py:20
  (14 other events, 105.5 us)
